TPU v7x, 128 devices: a whole 4x4x4 slice. The times are simulated.
128 devices in a mesh: ty: 8 (over x_lo, y), tx: 16 (over z, x_hi, core).
Axes of the slice: x: 4 (x_hi: 2, x_lo: 2; x = x_hi * 2 + x_lo), y: 4, z: 4, core: 2. Of those that a mesh axis runs over, the one named last changes fastest.
Arguments:
- object_slices: float32 [2, 2, 2048, 4096], P(None, None, 'ty', 'tx'), may hold values from -5 to 5
- probe: float32 [2, 256, 256], replicated, may hold values from -5 to 5
- position_count: int32 [8, 16], P('ty', 'tx'), may hold values from 1 to 5, as said below
- offsets: int32 [8, 16, 5, 2], P('ty', 'tx'), may hold values from 0 to 128
- intensities: float32 [8, 16, 5, 256, 256], P('ty', 'tx'), may hold values from 0 to 2
Outputs:
- object_new: float32 [2, 2, 2048, 4096], P(None, None, 'ty', 'tx')
- probe_new: float32 [2, 256, 256], replicated
Inputs may be any that keep to these rules, and one draw needn't show every extreme that they name: `position_count`: each tile has 1 to 5 positions; some tile has exactly 5.
All inputs are finite; a program needn't handle non-finite values.
Results may differ from a plain program's by a relative error of at most 0.0003.
Values sent between devices are 32-bit elements; how exact they have to be, the bound alone decides.
A program may use at most 128 MiB of HBM per device.

v0:
```python
import math

import jax
import jax.numpy as jnp
from jax import lax
from jax.sharding import PartitionSpec as P

PROBE = 256
CORE = 256
MARGIN = 64
ITERS = 2


chirp_rate = 0.5
object_rate = 0.5
probe_rate = 2.0


def extended_2(block, sides, width):
    for axis, dim in sides:
        count = lax.axis_size(axis)
        forward = [(i, i + 1) for i in range(count - 1)]
        forward.append((count - 1, 0))
        backward = [(target, source) for source, target in forward]
        low = lax.ppermute(
            lax.slice_in_dim(block, block.shape[dim] - width, None, axis=dim), axis, forward
        )
        high = lax.ppermute(lax.slice_in_dim(block, 0, width, axis=dim), axis, backward)
        block = jnp.concatenate([low, block, high], axis=dim)
    return block


def matmul(left, right):
    return jnp.dot(left, right, precision=lax.Precision.HIGHEST, preferred_element_type=jnp.float32)


def complex_product(left_real, left_imag, right_real, right_imag):
    out_real = matmul(left_real, right_real) - matmul(left_imag, right_imag)
    out_imag = matmul(left_real, right_imag) + matmul(left_imag, right_real)
    return (out_real, out_imag)


def dft_tables(size):
    index = lax.iota(jnp.int32, size)
    product = index[:, None] * index[None, :] % size
    angles = product.astype(jnp.float32) * (2.0 * math.pi / size)
    factor = 1.0 / math.sqrt(size)
    four_real = jnp.cos(angles) * factor
    four_imag = -jnp.sin(angles) * factor
    centred = ((index + size // 2) % size - size // 2).astype(jnp.float32)
    phases = centred * centred * (chirp_rate * math.pi / size)
    kernel_real = jnp.cos(phases)
    kernel_imag = -jnp.sin(phases)
    scaled_real = four_real * kernel_real[None, :] + four_imag * kernel_imag[None, :]
    scaled_imag = four_real * kernel_imag[None, :] - four_imag * kernel_real[None, :]
    prop_real, prop_imag = complex_product(scaled_real, scaled_imag, four_real, four_imag)
    return (four_real, four_imag, prop_real, prop_imag)


def forward_pair(mat_real, mat_imag, field_real, field_imag):
    mid_real, mid_imag = complex_product(mat_real, mat_imag, field_real, field_imag)
    return complex_product(mid_real, mid_imag, mat_real.T, mat_imag.T)


def adjoint_pair(mat_real, mat_imag, field_real, field_imag):
    mid_real, mid_imag = complex_product(mat_real.T, -mat_imag.T, field_real, field_imag)
    return complex_product(mid_real, mid_imag, mat_real, -mat_imag)


def position_grad(probe_now, window, measured, tables):
    four_real, four_imag, prop_real, prop_imag = tables
    probe_real, probe_imag = (probe_now[0], probe_now[1])
    one_real, one_imag, two_real, two_imag = (window[0], window[1], window[2], window[3])
    wave_real = probe_real * one_real - probe_imag * one_imag
    wave_imag = probe_real * one_imag + probe_imag * one_real
    moved_real, moved_imag = forward_pair(prop_real, prop_imag, wave_real, wave_imag)
    exit_real = moved_real * two_real - moved_imag * two_imag
    exit_imag = moved_real * two_imag + moved_imag * two_real
    far_real, far_imag = forward_pair(four_real, four_imag, exit_real, exit_imag)
    misfit = far_real * far_real + far_imag * far_imag - measured
    back_real, back_imag = adjoint_pair(four_real, four_imag, misfit * far_real, misfit * far_imag)
    grad_two_real = moved_real * back_real + moved_imag * back_imag
    grad_two_imag = moved_real * back_imag - moved_imag * back_real
    gmove_real = two_real * back_real + two_imag * back_imag
    gmove_imag = two_real * back_imag - two_imag * back_real
    gwave_real, gwave_imag = adjoint_pair(prop_real, prop_imag, gmove_real, gmove_imag)
    grad_one_real = probe_real * gwave_real + probe_imag * gwave_imag
    grad_one_imag = probe_real * gwave_imag - probe_imag * gwave_real
    gprobe_real = one_real * gwave_real + one_imag * gwave_imag
    gprobe_imag = one_real * gwave_imag - one_imag * gwave_real
    object_part = jnp.stack([grad_one_real, grad_one_imag, grad_two_real, grad_two_imag])
    return (object_part, jnp.stack([gprobe_real, gprobe_imag]))


def fold_axis(padded, width, dim):
    extent = padded.shape[dim] - 2 * width
    middle = lax.slice_in_dim(padded, width, width + extent, axis=dim)
    before = lax.slice_in_dim(padded, 0, width, axis=dim)
    after = lax.slice_in_dim(padded, width + extent, extent + 2 * width, axis=dim)
    spec_before = [(0, 0)] * padded.ndim
    spec_before[dim] = (2 * MARGIN - width, extent - 2 * MARGIN)
    spec_after = [(0, 0)] * padded.ndim
    spec_after[dim] = (CORE, extent - CORE - width)
    return middle + jnp.pad(before, spec_before) + jnp.pad(after, spec_after)


def fold_sums(padded, width):
    return fold_axis(fold_axis(padded, width, 1), width, 2)


def body(object_slices, probe, position_count, offsets, intensities):
    tables = dft_tables(PROBE)
    extent = CORE + 2 * MARGIN
    zero = jnp.int32(0)
    count = position_count[0, 0]
    core = object_slices.reshape(4, CORE, CORE)
    extended = extended_2(core, (("ty", 1), ("tx", 2)), MARGIN)
    probe_now = probe
    devices = lax.axis_size("ty") * lax.axis_size("tx")
    for step in range(ITERS):

        def visit(slot, carry):
            local, local_probe = carry
            top = offsets[0, 0, slot, 0]
            left = offsets[0, 0, slot, 1]
            window = lax.dynamic_slice(extended, (zero, top, left), (4, PROBE, PROBE))
            object_part, probe_part = position_grad(
                probe_now, window, intensities[0, 0, slot], tables
            )
            current = lax.dynamic_slice(local, (zero, top, left), (4, PROBE, PROBE))
            local = lax.dynamic_update_slice(local, current + object_part, (zero, top, left))
            return (local, local_probe + probe_part)

        start = (
            jnp.zeros((4, extent, extent), jnp.float32),
            jnp.zeros((2, PROBE, PROBE), jnp.float32),
        )
        grads, probe_grad = lax.fori_loop(zero, count, visit, start)
        peak = jnp.max(probe_now[0] * probe_now[0] + probe_now[1] * probe_now[1]) + 1e-06
        padded = extended_2(grads, (("ty", 1), ("tx", 2)), MARGIN)
        total = fold_sums(padded, MARGIN)[:, MARGIN : MARGIN + CORE, MARGIN : MARGIN + CORE]
        core = core - object_rate / peak * total
        if step + 1 < ITERS:
            extended = extended_2(core, (("ty", 1), ("tx", 2)), MARGIN)
        summed = lax.psum(probe_grad, ("ty", "tx"))
        probe_now = probe_now - probe_rate / devices * summed
    return (core.reshape(2, 2, CORE, CORE), probe_now)


def solution(mesh):
    placed = (
        P(None, None, "ty", "tx"),
        P(),
        P("ty", "tx"),
        P("ty", "tx", None, None),
        P("ty", "tx", None, None, None),
    )
    return jax.shard_map(
        body,
        mesh=mesh,
        in_specs=placed,
        out_specs=(P(None, None, "ty", "tx"), P()),
        check_vma=False,
    )
```

profile of v0, /device:TPU:1, one launch (start us, length us, event | category | flops | bytes accessed | tf_op | source)
XLA Modules:
  0.0 1056.5 jit_solution(428743954440561361)
XLA Ops:
  10.0 2.1 collective-permute-start
  12.2 2.4 collective-permute-start.1
  17.7 8.6 collective-permute-done
  26.6 4.0 collective-permute-start.2
  33.6 2.9 collective-permute-done.2
  36.4 5.2 collective-permute-done.3
  41.6 3.1 pad_maximum_fusion.2
  47.1 262.4 %while.32 = (s32[]{:T(128)}, f32[4,384,384]{2,1,0:T(8,128)}, f32[2,256,256]{2,1,0:T(8,128)}, s32[]{:T(128)}, s32[1,1,5,2]{2,3,1,0:T(2,128)S(1)}, /*index=5*/f32[...) while((s32[]{:T(128)}, f32[4,384,384]{2,1,0:T(8,128)}, ...), condition=%wide.region_2.3_spmd.clone.clone, body=%wide.region_1.2_spmd.clone.clone.sunk | while | flops 6464077824 | bytes 48234916 | solution.py:138
  75.9 2.5 fusion.635
  96.2 2.4 fusion.646
  115.6 2.0 maximum_add_fusion.8
  117.6 11.1 %dynamic_update_slice.16 = f32[4,384,384]{2,1,0:T(8,128)} dynamic-update-slice(f32[4,384,384]{2,1,0:T(8,128)} %get-tuple-element.1014, f32[4,256,256]{2,1,0:T(8,128)S(1)} %maximum_add_fusion.8, s32[]{:T(128)} %constant.70.clone.1..sunk, s32[]{:T(128)S(6)} %select_n.366, s32[]{:T(128)S(6)} %select_n.367) | dynamic-update-slice | bytes 2097156 | tf_op jit(solution)/shard_map/while/body/dynamic_update_slice | solution.py:131
  133.5 2.5 fusion.635
  153.8 2.4 fusion.646
  173.2 2.0 maximum_add_fusion.8
  175.2 11.5 %dynamic_update_slice.16 = f32[4,384,384]{2,1,0:T(8,128)} dynamic-update-slice(f32[4,384,384]{2,1,0:T(8,128)} %get-tuple-element.1014, f32[4,256,256]{2,1,0:T(8,128)S(1)} %maximum_add_fusion.8, s32[]{:T(128)} %constant.70.clone.1..sunk, s32[]{:T(128)S(6)} %select_n.366, s32[]{:T(128)S(6)} %select_n.367) | dynamic-update-slice | bytes 2097156 | tf_op jit(solution)/shard_map/while/body/dynamic_update_slice | solution.py:131
  191.6 2.5 fusion.635
  211.8 2.4 fusion.646
  231.3 2.0 maximum_add_fusion.8
  233.3 11.1 %dynamic_update_slice.16 = f32[4,384,384]{2,1,0:T(8,128)} dynamic-update-slice(f32[4,384,384]{2,1,0:T(8,128)} %get-tuple-element.1014, f32[4,256,256]{2,1,0:T(8,128)S(1)} %maximum_add_fusion.8, s32[]{:T(128)} %constant.70.clone.1..sunk, s32[]{:T(128)S(6)} %select_n.366, s32[]{:T(128)S(6)} %select_n.367) | dynamic-update-slice | bytes 2097156 | tf_op jit(solution)/shard_map/while/body/dynamic_update_slice | solution.py:131
  249.3 2.5 fusion.635
  269.5 2.4 fusion.646
  289.0 2.0 maximum_add_fusion.8
  291.0 11.6 %dynamic_update_slice.16 = f32[4,384,384]{2,1,0:T(8,128)} dynamic-update-slice(f32[4,384,384]{2,1,0:T(8,128)} %get-tuple-element.1014, f32[4,256,256]{2,1,0:T(8,128)S(1)} %maximum_add_fusion.8, s32[]{:T(128)} %constant.70.clone.1..sunk, s32[]{:T(128)S(6)} %select_n.366, s32[]{:T(128)S(6)} %select_n.367) | dynamic-update-slice | bytes 2097156 | tf_op jit(solution)/shard_map/while/body/dynamic_update_slice | solution.py:131
  310.8 3.6 collective-permute-start.5
  314.4 3.1 copy.25
  317.5 2.2 collective-permute-done.4
  320.9 55.3 %collective-permute-done.5 = f32[4,64,384]{2,1,0:T(8,128)S(1)} collective-permute-done((f32[4,64,384]{2,1,0:T(8,128)S(1)}, f32[4,64,384]{2,1,0:T(8,128)S(1)}, u32[]{:S(2)}, u32[]{:S(2)}) %collective-permute-start.5) | collective-permute-done | bytes 393248 | tf_op jit(solution)/shard_map/ppermute | solution.py:28
  376.5 2.5 pad_maximum_fusion.9
  379.0 2.3 collective-permute-start.7
  382.6 2.8 collective-permute-done.6
  385.4 6.9 collective-permute-done.7
  392.3 3.0 pad_maximum_fusion
  395.4 2.8 fusion.242
  401.2 5.1 collective-permute-start.8
  406.4 10.2 collective-permute-done.8
  416.6 1.9 collective-permute-done.9
  418.5 2.2 pad_maximum_fusion.12
  420.7 2.5 collective-permute-start.11
  423.2 134.6 %all-reduce.11.cloned.1.call-done = f32[2,256,256]{2,1,0:T(8,128)} async-done(((f32[2,256,256]{2,1,0:T(8,128)}), f32[2,256,256]{2,1,0:T(8,128)}) %all-reduce.11.cloned.1.call-update) | async-done | bytes 524304 | tf_op jit(solution)/shard_map/psum | solution.py:145
  558.9 3.3 pad_maximum_fusion.3
  564.6 263.0 %while.33 = (s32[]{:T(128)}, f32[4,384,384]{2,1,0:T(8,128)}, f32[2,256,256]{2,1,0:T(8,128)}, s32[]{:T(128)}, s32[1,1,5,2]{2,3,1,0:T(2,128)S(1)}, /*index=5*/f32[...) while((s32[]{:T(128)}, f32[4,384,384]{2,1,0:T(8,128)}, ...), condition=%wide.region_6.7_spmd.clone.clone, body=%wide.region_5.6_spmd.clone.clone.sunk | while | flops 6464077824 | bytes 48234916 | solution.py:138
  593.3 2.5 fusion.709
  613.5 2.4 fusion.720
  633.8 1.8 maximum_add_fusion.10
  635.6 11.1 %dynamic_update_slice.17 = f32[4,384,384]{2,1,0:T(8,128)} dynamic-update-slice(f32[4,384,384]{2,1,0:T(8,128)} %get-tuple-element.1071, f32[4,256,256]{2,1,0:T(8,128)S(1)} %maximum_add_fusion.10, s32[]{:T(128)} %constant.70.clone.1..sunk.1, s32[]{:T(128)S(6)} %select_n.385, s32[]{:T(128)S(6)} %select_n.386) | dynamic-update-slice | bytes 2097156 | tf_op jit(solution)/shard_map/while/body/dynamic_update_slice | solution.py:131
  651.5 2.5 fusion.709
  671.8 2.4 fusion.720
  693.8 11.5 %dynamic_update_slice.17 = f32[4,384,384]{2,1,0:T(8,128)} dynamic-update-slice(f32[4,384,384]{2,1,0:T(8,128)} %get-tuple-element.1071, f32[4,256,256]{2,1,0:T(8,128)S(1)} %maximum_add_fusion.10, s32[]{:T(128)} %constant.70.clone.1..sunk.1, s32[]{:T(128)S(6)} %select_n.385, s32[]{:T(128)S(6)} %select_n.386) | dynamic-update-slice | bytes 2097156 | tf_op jit(solution)/shard_map/while/body/dynamic_update_slice | solution.py:131
  710.1 2.5 fusion.709
  730.4 2.4 fusion.720
  752.4 11.1 %dynamic_update_slice.17 = f32[4,384,384]{2,1,0:T(8,128)} dynamic-update-slice(f32[4,384,384]{2,1,0:T(8,128)} %get-tuple-element.1071, f32[4,256,256]{2,1,0:T(8,128)S(1)} %maximum_add_fusion.10, s32[]{:T(128)} %constant.70.clone.1..sunk.1, s32[]{:T(128)S(6)} %select_n.385, s32[]{:T(128)S(6)} %select_n.386) | dynamic-update-slice | bytes 2097156 | tf_op jit(solution)/shard_map/while/body/dynamic_update_slice | solution.py:131
  768.4 2.5 fusion.709
  788.6 2.4 fusion.720
  810.7 11.6 %dynamic_update_slice.17 = f32[4,384,384]{2,1,0:T(8,128)} dynamic-update-slice(f32[4,384,384]{2,1,0:T(8,128)} %get-tuple-element.1071, f32[4,256,256]{2,1,0:T(8,128)S(1)} %maximum_add_fusion.10, s32[]{:T(128)} %constant.70.clone.1..sunk.1, s32[]{:T(128)S(6)} %select_n.385, s32[]{:T(128)S(6)} %select_n.386) | dynamic-update-slice | bytes 2097156 | tf_op jit(solution)/shard_map/while/body/dynamic_update_slice | solution.py:131
  828.8 3.6 collective-permute-start.13
  832.4 3.1 copy.30
  835.5 2.1 collective-permute-done.12
  837.8 55.3 %collective-permute-done.13 = f32[4,64,384]{2,1,0:T(8,128)S(1)} collective-permute-done((f32[4,64,384]{2,1,0:T(8,128)S(1)}, f32[4,64,384]{2,1,0:T(8,128)S(1)}, u32[]{:S(2)}, u32[]{:S(2)}) %collective-permute-start.13) | collective-permute-done | bytes 393248 | tf_op jit(solution)/shard_map/ppermute | solution.py:28
  893.4 2.5 pad_maximum_fusion.6
  895.9 4.3 collective-permute-start.15
  901.6 138.4 %all-reduce.13.cloned.1.call-done = f32[2,256,256]{2,1,0:T(8,128)} async-done(((f32[2,256,256]{2,1,0:T(8,128)}), f32[2,256,256]{2,1,0:T(8,128)}) %all-reduce.13.cloned.1.call-update) | async-done | bytes 524304 | tf_op jit(solution)/shard_map/psum | solution.py:145
  1040.0 1.9 multiply_subtract_fusion
  1041.9 2.9 pad_maximum_fusion.1
  (407 shorter events, 317.6 us)
Async XLA Ops:
  7.2 550.5 %all-reduce.11.cloned.1.call-start = ((), (), s32[]{:S(2)}) async-start(), calls=%async_computation | async-start | bytes 1048576 | tf_op jit(solution)/shard_map/psum | solution.py:145
  8.8 32.9 %copy-start.3 = (f32[2,2,256,256]{2,3,1,0:T(8,128)}, f32[2,2,256,256]{2,3,1,0:T(8,128)S(1)}, u32[]{:S(2)}) copy-start(f32[2,2,256,256]{2,3,1,0:T(8,128)S(1)} %copy.21) | copy-start | bytes 3145732
  10.0 16.2 %collective-permute-start = (f32[4,64,256]{1,2,0:T(8,128)}, f32[4,64,256]{1,2,0:T(8,128)S(1)}, u32[]{:S(2)}, u32[]{:S(2)}) collective-permute-start(f32[4,64,256]{1,2,0:T(8,128)} %get-tuple-element.756), channel_id=1, source_target_pairs={{0,16},{16,32},{32,48},{48,64},{64,80},{80,96},{96,112},{112,0},{1... | collective-permute-start | bytes 786440 | tf_op jit(solution)/shard_map/ppermute | solution.py:25
  12.2 14.1 %collective-permute-start.1 = (f32[4,64,256]{1,2,0:T(8,128)}, f32[4,64,256]{1,2,0:T(8,128)S(1)}, u32[]{:S(2)}, u32[]{:S(2)}) collective-permute-start(f32[4,64,256]{1,2,0:T(8,128)} %get-tuple-element.757), channel_id=1, source_target_pairs={{16,0},{32,16},{48,32},{64,48},{80,64},{96,80},{112,96},{0,112},{1... | collective-permute-start | bytes 786440 | tf_op jit(solution)/shard_map/ppermute | solution.py:28
  26.3 5.8 copy-start.12
  26.6 9.8 collective-permute-start.2
  30.6 11.0 %collective-permute-start.3 = (f32[4,384,64]{1,2,0:T(8,128)S(1)}, f32[4,384,64]{1,2,0:T(8,128)S(1)}, u32[]{:S(2)}, u32[]{:S(2)}) collective-permute-start(f32[4,384,64]{1,2,0:T(8,128)S(1)} %get-tuple-element.753), channel_id=1, source_target_pairs={{1,0},{2,1},{3,2},{4,3},{5,4},{6,5},{7,6},{8,7},{9,8},{10,9},{11,1... | collective-permute-start | bytes 1179656 | tf_op jit(solution)/shard_map/ppermute | solution.py:28
  33.5 13.6 %copy-start = (f32[2,256,256]{2,1,0:T(8,128)S(1)}, f32[2,256,256]{2,1,0:T(8,128)}, u32[]{:S(2)}) copy-start(f32[2,256,256]{2,1,0:T(8,128)} %param.10) | copy-start | bytes 1572868
  33.5 13.6 %copy-start.13 = (s32[1,1,5,2]{2,3,1,0:T(2,128)S(1)}, s32[1,1,5,2]{2,3,1,0:T(2,128)}, u32[]{:S(2)}) copy-start(s32[1,1,5,2]{2,3,1,0:T(2,128)} %param.12) | copy-start | bytes 124
  112.3 3.1 copy-start.9
  115.6 13.1 %copy-start.10 = (f32[2,256,256]{2,1,0:T(8,128)}, f32[2,256,256]{2,1,0:T(8,128)S(1)}, u32[]{:S(2)}) copy-start(f32[2,256,256]{2,1,0:T(8,128)S(1)} %maximum_add_fusion.9) | copy-start | bytes 1572868 | tf_op jit(solution)/shard_map/while
  170.0 3.1 copy-start.9
  173.2 13.5 %copy-start.10 = (f32[2,256,256]{2,1,0:T(8,128)}, f32[2,256,256]{2,1,0:T(8,128)S(1)}, u32[]{:S(2)}) copy-start(f32[2,256,256]{2,1,0:T(8,128)S(1)} %maximum_add_fusion.9) | copy-start | bytes 1572868 | tf_op jit(solution)/shard_map/while
  228.0 3.1 copy-start.9
  231.3 13.1 %copy-start.10 = (f32[2,256,256]{2,1,0:T(8,128)}, f32[2,256,256]{2,1,0:T(8,128)S(1)}, u32[]{:S(2)}) copy-start(f32[2,256,256]{2,1,0:T(8,128)S(1)} %maximum_add_fusion.9) | copy-start | bytes 1572868 | tf_op jit(solution)/shard_map/while
  285.7 3.1 copy-start.9
  288.9 13.6 %copy-start.10 = (f32[2,256,256]{2,1,0:T(8,128)}, f32[2,256,256]{2,1,0:T(8,128)S(1)}, u32[]{:S(2)}) copy-start(f32[2,256,256]{2,1,0:T(8,128)S(1)} %maximum_add_fusion.9) | copy-start | bytes 1572868 | tf_op jit(solution)/shard_map/while
  310.8 8.9 collective-permute-start.4
  310.8 65.4 %collective-permute-start.5 = (f32[4,64,384]{2,1,0:T(8,128)S(1)}, f32[4,64,384]{2,1,0:T(8,128)S(1)}, u32[]{:S(2)}, u32[]{:S(2)}) collective-permute-start(f32[4,64,384]{2,1,0:T(8,128)S(1)} %get-tuple-element.749), channel_id=1, source_target_pairs={{16,0},{32,16},{48,32},{64,48},{80,64},{96,80},{112,96},{0,112},{1... | collective-permute-start | bytes 1179656 | tf_op jit(solution)/shard_map/ppermute | solution.py:28
  379.0 6.4 collective-permute-start.6
  379.0 13.3 %collective-permute-start.7 = (f32[4,512,64]{1,2,0:T(8,128)}, f32[4,512,64]{1,2,0:T(8,128)}, u32[]{:S(2)}, u32[]{:S(2)}) collective-permute-start(f32[4,512,64]{1,2,0:T(8,128)} %get-tuple-element.741), channel_id=1, source_target_pairs={{1,0},{2,1},{3,2},{4,3},{5,4},{6,5},{7,6},{8,7},{9,8},{10,9},{11,1... | collective-permute-start | bytes 1572872 | tf_op jit(solution)/shard_map/ppermute | solution.py:28
  382.6 12.8 %copy-start.2 = (f32[4,384,384]{1,2,0:T(8,128)S(1)}, f32[4,384,384]{1,2,0:T(8,128)}, u32[]{:S(2)}) copy-start(f32[4,384,384]{1,2,0:T(8,128)} %copy.25) | copy-start | bytes 7077892
  398.2 1.2 copy-start.4
  399.9 158.9 %copy-start.5 = (f32[4,256,256]{1,2,0:T(8,128)}, f32[4,256,256]{1,2,0:T(8,128)S(1)}, u32[]{:S(2)}) copy-start(f32[4,256,256]{1,2,0:T(8,128)S(1)} %fusion.249) | copy-start | bytes 3145732
  401.2 15.3 %collective-permute-start.8 = (f32[4,64,256]{1,2,0:T(8,128)}, f32[4,64,256]{1,2,0:T(8,128)S(1)}, u32[]{:S(2)}, u32[]{:S(2)}) collective-permute-start(f32[4,64,256]{1,2,0:T(8,128)} %get-tuple-element.754), channel_id=1, source_target_pairs={{0,16},{16,32},{32,48},{48,64},{64,80},{80,96},{96,112},{112,0},{1... | collective-permute-start | bytes 786440 | tf_op jit(solution)/shard_map/ppermute | solution.py:25
  406.3 12.2 %collective-permute-start.9 = (f32[4,64,256]{1,2,0:T(8,128)}, f32[4,64,256]{1,2,0:T(8,128)}, u32[]{:S(2)}, u32[]{:S(2)}) collective-permute-start(f32[4,64,256]{1,2,0:T(8,128)} %get-tuple-element.755), channel_id=1, source_target_pairs={{16,0},{32,16},{48,32},{64,48},{80,64},{96,80},{112,96},{0,112},{1... | collective-permute-start | bytes 786440 | tf_op jit(solution)/shard_map/ppermute | solution.py:28
  406.3 633.7 %all-reduce.13.cloned.1.call-start = ((), (), s32[]{:S(2)}) async-start(), calls=%async_computation.1 | async-start | bytes 1048576 | tf_op jit(solution)/shard_map/psum | solution.py:145
  416.5 6.6 copy-start.11
  420.7 138.2 %collective-permute-start.10 = (f32[4,384,64]{1,2,0:T(8,128)}, f32[4,384,64]{1,2,0:T(8,128)S(1)}, u32[]{:S(2)}, u32[]{:S(2)}) collective-permute-start(f32[4,384,64]{1,2,0:T(8,128)} %get-tuple-element.750), channel_id=1, source_target_pairs={{0,1},{1,2},{2,3},{3,4},{4,5},{5,6},{6,7},{7,8},{8,9},{9,10},{10,1... | collective-permute-start | bytes 1179656 | tf_op jit(solution)/shard_map/ppermute | solution.py:25
  420.7 138.2 %collective-permute-start.11 = (f32[4,384,64]{1,2,0:T(8,128)}, f32[4,384,64]{1,2,0:T(8,128)}, u32[]{:S(2)}, u32[]{:S(2)}) collective-permute-start(f32[4,384,64]{1,2,0:T(8,128)} %get-tuple-element.751), channel_id=1, source_target_pairs={{1,0},{2,1},{3,2},{4,3},{5,4},{6,5},{7,6},{8,7},{9,8},{10,9},{11,1... | collective-permute-start | bytes 1179656 | tf_op jit(solution)/shard_map/ppermute | solution.py:28
  629.7 3.1 copy-start.7
  633.0 0.8 copy-start.8
  687.9 3.1 copy-start.7
  691.2 0.8 copy-start.8
  746.5 3.1 copy-start.7
  749.8 0.8 copy-start.8
  804.8 3.1 copy-start.7
  808.1 0.8 copy-start.8
  828.8 8.8 collective-permute-start.12
  828.8 64.3 %collective-permute-start.13 = (f32[4,64,384]{2,1,0:T(8,128)S(1)}, f32[4,64,384]{2,1,0:T(8,128)S(1)}, u32[]{:S(2)}, u32[]{:S(2)}) collective-permute-start(f32[4,64,384]{2,1,0:T(8,128)S(1)} %get-tuple-element.747), channel_id=1, source_target_pairs={{16,0},{32,16},{48,32},{64,48},{80,64},{96,80},{112,96},{0,112},{1... | collective-permute-start | bytes 1179656 | tf_op jit(solution)/shard_map/ppermute | solution.py:28
  895.9 146.0 %collective-permute-start.14 = (f32[4,512,64]{1,2,0:T(8,128)}, f32[4,512,64]{1,2,0:T(8,128)S(1)}, u32[]{:S(2)}, u32[]{:S(2)}) collective-permute-start(f32[4,512,64]{1,2,0:T(8,128)} %get-tuple-element.738), channel_id=1, source_target_pairs={{0,1},{1,2},{2,3},{3,4},{4,5},{5,6},{6,7},{7,8},{8,9},{9,10},{10,1... | collective-permute-start | bytes 1572872 | tf_op jit(solution)/shard_map/ppermute | solution.py:25
  895.9 146.0 %collective-permute-start.15 = (f32[4,512,64]{1,2,0:T(8,128)}, f32[4,512,64]{1,2,0:T(8,128)S(1)}, u32[]{:S(2)}, u32[]{:S(2)}) collective-permute-start(f32[4,512,64]{1,2,0:T(8,128)} %get-tuple-element.739), channel_id=1, source_target_pairs={{1,0},{2,1},{3,2},{4,3},{5,4},{6,5},{7,6},{8,7},{9,8},{10,9},{11,1... | collective-permute-start | bytes 1572872 | tf_op jit(solution)/shard_map/ppermute | solution.py:28
  1041.9 3.0 copy-start.1
  1046.5 1.2 copy-start.6
Sparse Core Ops, SparseCore 0:
  406.4 151.2 all-reduce.10
  835.6 204.3 all-reduce.12
where the time goes:
time: 1070 us; the launch traced here: 1060 us
  waiting for transfers between devices  426 us (40%)
  matrix products  280 us (26%)
  local copies, waits for them, and re-layouts  162 us (15%)
  loops' own time  96.4 us (9%)
  other arithmetic  46.5 us (4%)
  starting transfers between devices  30 us (3%)
  between operations  15.9 us (1%)
    dot_general x260, matrix products, matmul(): jnp.dot(left, right, precision=lax.Precision.HIGHEST, preferred_element_t...  280 us
    psum x2, waiting for transfers between devices, body(): summed = lax.psum(probe_grad, ('ty', 'tx'))  273 us
    ppermute x8, waiting for transfers between devices, extended_2(): lax.ppermute(lax.slice_in_dim(block, 0, width, axis=dim), axis, backward)  125 us
    another operation x2, loops' own time, body(): grads, probe_grad = lax.fori_loop(zero, count, visit, start)  96.4 us
    dynamic_update_slice x8, local copies, waits for them, and re-layouts, visit(): lax.dynamic_update_slice(local, current + object_part, (zero, top, left))  90.6 us
    ppermute x8, waiting for transfers between devices, extended_2(): lax.ppermute(lax.slice_in_dim(block, block.shape[dim] - width, None, axis...  28.7 us
    while x64, local copies, waits for them, and re-layouts  22.5 us
  transfers between devices with their start and end apart: 18, of which 13 were waited for; matrix products, arithmetic and copies ran while one was open for 2% of the time, Pallas kernels for 0%

commit v1 on v0

v1 whole, which is shorter than its diff:
```python
import functools

import jax
import jax.numpy as jnp
import ml_dtypes
import numpy as np
from jax import lax
from jax.experimental import pallas as pl
from jax.experimental.pallas import tpu as pltpu
from jax.sharding import PartitionSpec as P

PROBE = 256
MAXPOS = 5
ITERS = 2
bf = jnp.bfloat16
f32 = jnp.float32

chirp_rate = 0.5
object_rate = 0.5
probe_rate = 2.0


def tables():
    n = PROBE
    k = np.arange(n)
    four = np.exp(-2j * np.pi * ((k[:, None] * k[None, :]) % n) / n) / np.sqrt(n)
    c = (((k + n // 2) % n) - n // 2).astype(np.float64)
    prop = (np.conj(four) * np.exp(-1j * chirp_rate * np.pi * c * c / n)[None, :]) @ four
    out = []
    for mat in (four, prop):
        real, imag = mat.real, mat.imag
        for part in (real, imag - real, real + imag):
            part = part.astype(np.float32)
            high = part.astype(ml_dtypes.bfloat16)
            out += [high, (part - high.astype(np.float32)).astype(ml_dtypes.bfloat16)]
    return np.stack(out).reshape(2, 3, 2, n, n)


def split(x):
    high = x.astype(bf)
    return high, (x - high.astype(f32)).astype(bf)


def dot(a, b):
    return jnp.dot(a, b, preferred_element_type=f32)


def left(tab, which, j, x):
    high, low = split(x)
    mat = jnp.concatenate([tab[which, j, 0], tab[which, j, 0], tab[which, j, 1]], axis=1)
    return dot(mat, jnp.concatenate([high, low, high], axis=0))


def right(tab, which, j, x):
    high, low = split(x)
    mat = jnp.concatenate([tab[which, j, 0], tab[which, j, 0], tab[which, j, 1]], axis=0)
    return dot(jnp.concatenate([high, low, high], axis=1), mat)


def sandwich(tab, which, real, imag, mid):
    shared = left(tab, which, 0, real + imag)
    mid[1] = shared + left(tab, which, 1, real)
    mid[0] = shared - left(tab, which, 2, imag)
    real, imag = mid[0], mid[1]
    shared = right(tab, which, 0, real + imag)
    return shared - right(tab, which, 2, imag), shared + right(tab, which, 1, real)


def compute_kernel(count_ref, off_ref, ext_ref, probe_ref, int_ref, tab, g_ref, gp_ref, win, moved, mid):
    g_ref[...] = jnp.zeros_like(g_ref)
    gp_ref[...] = jnp.zeros_like(gp_ref)
    lane = lax.broadcasted_iota(jnp.int32, (256, 128), 1)

    def visit(s, carry):
        top, left_col = off_ref[s, 0], off_ref[s, 1]
        inner = left_col >= 64
        t0 = jnp.where(inner, 0, 2)
        t1 = jnp.where(inner, 1, 0)
        t2 = jnp.where(inner, 2, 1)
        shift = jnp.where(inner, left_col - 64, left_col + 64)
        keep = lane < 128 - shift
        rows = pl.ds(top, 256)
        for p in range(4):
            a, b, c = [pltpu.roll(ext_ref[p, t, rows, :], 128 - shift, 1) for t in (t0, t1, t2)]
            win[p, :, 0:128] = jnp.where(keep, a, b)
            win[p, :, 128:256] = jnp.where(keep, b, c)
        pr, pi = probe_ref[0], probe_ref[1]
        moved[0], moved[1] = sandwich(tab, 1, pr * win[0] - pi * win[1], pr * win[1] + pi * win[0], mid)
        er = moved[0] * win[2] - moved[1] * win[3]
        ei = moved[0] * win[3] + moved[1] * win[2]
        fr, fi = sandwich(tab, 0, er, ei, mid)
        misfit = fr * fr + fi * fi - int_ref[s]
        cr, ci = sandwich(tab, 0, misfit * fr, -(misfit * fi), mid)
        g2r = moved[0] * cr - moved[1] * ci
        g2i = -(moved[0] * ci + moved[1] * cr)
        wr, wi = sandwich(tab, 1, win[2] * cr - win[3] * ci, win[2] * ci + win[3] * cr, mid)
        g1r = probe_ref[0] * wr - probe_ref[1] * wi
        g1i = -(probe_ref[0] * wi + probe_ref[1] * wr)
        for h, gp in enumerate((win[0] * wr - win[1] * wi, -(win[0] * wi + win[1] * wr))):
            gp_ref[h, 0] += gp[:, 0:128]
            gp_ref[h, 1] += gp[:, 128:256]
        before = lane < shift
        for p, g in enumerate((g1r, g1i, g2r, g2i)):
            a, b = pltpu.roll(g[:, 0:128], shift, 1), pltpu.roll(g[:, 128:256], shift, 1)
            g_ref[p, t0, rows, :] += jnp.where(before, 0.0, a)
            g_ref[p, t1, rows, :] += jnp.where(before, a, b)
            g_ref[p, t2, rows, :] += jnp.where(before, b, 0.0)
        return carry

    lax.fori_loop(0, count_ref[0], visit, 0)


def compute(count, off, ext, probe, inten, tab):
    vmem = pl.BlockSpec(memory_space=pltpu.VMEM)
    smem = pl.BlockSpec(memory_space=pltpu.SMEM)
    return pl.pallas_call(
        compute_kernel,
        out_shape=(jax.ShapeDtypeStruct((4, 3, 384, 128), f32), jax.ShapeDtypeStruct((2, 2, 256, 128), f32)),
        in_specs=[smem, smem, vmem, vmem, vmem, vmem],
        out_specs=(vmem, vmem),
        scratch_shapes=[pltpu.VMEM((4, 256, 256), f32), pltpu.VMEM((2, 256, 256), f32), pltpu.VMEM((2, 256, 256), f32)],
        compiler_params=pltpu.CompilerParams(vmem_limit_bytes=40 << 20),
        name="positions",
    )(count, off, ext, probe, inten, tab)


NTY, NTX = 8, 16
MESH = pl.DeviceIdType.MESH
DIRS = [(dy, dx) for dy in (-1, 0, 1) for dx in (-1, 0, 1) if (dy, dx) != (0, 0)]
V = pl.BlockSpec(memory_space=pltpu.VMEM)


def half_lanes(shape):
    return lax.broadcasted_iota(jnp.int32, shape, len(shape) - 1) < 64


def pack(x, side):
    rows = x.shape[1] // 2
    first, second = x[:, :rows], x[:, rows:]
    low = half_lanes(first.shape)
    if side > 0:
        return jnp.where(low, pltpu.roll(first, 64, 2), second)
    return jnp.where(low, first, pltpu.roll(second, 64, 2))


def unpack(buf, side):
    turned = pltpu.roll(buf, 64, 2)
    pair = [turned, buf] if side > 0 else [buf, turned]
    return jnp.concatenate(pair, axis=1)


def keep_side(x, side):
    low = half_lanes(x.shape)
    return jnp.where(low, 0.0, x) if side > 0 else jnp.where(low, x, 0.0)


class Place:
    def __init__(self):
        self.ty, self.tx = lax.axis_index("ty"), lax.axis_index("tx")
        self.x_lo, self.y = self.ty // 4, lax.rem(self.ty, 4)
        self.z, self.core = self.tx // 4, lax.rem(self.tx, 2)
        self.x_hi = lax.rem(self.tx // 2, 2)
        self.x = self.x_hi * 2 + self.x_lo
        self.spot = self.y * 4 + self.z

    def neighbour(self, dy, dx):
        return (lax.rem(self.ty + dy + NTY, NTY), lax.rem(self.tx + dx + NTX, NTX))

    def sibling(self):
        return (self.ty, self.tx + 1 - 2 * self.core)

    def plane(self, k):
        y, z = lax.rem(self.y + k // 4, 4), lax.rem(self.z + lax.rem(k, 4), 4)
        return y * 4 + z, (self.x_lo * 4 + y, z * 4 + self.x_hi * 2 + self.core)

    def column(self, k):
        x = lax.rem(self.x + k, 4)
        return x, (lax.rem(x, 2) * 4 + self.y, self.z * 4 + (x // 2) * 2 + self.core)


def remote(src, dst, send, recv, device):
    return pltpu.make_async_remote_copy(
        src_ref=src, dst_ref=dst, send_sem=send, recv_sem=recv, device_id=device, device_id_type=MESH
    )


class Edges:
    def __init__(self, place, rows, cols, corners, sems):
        self.place, self.rows, self.cols, self.corners = place, rows, cols, corners
        self.send, self.recv = sems

    def slot(self, bufs, dy, dx):
        if dx == 0:
            return bufs[0].at[(dy + 1) // 2]
        if dy == 0:
            return bufs[1].at[(dx + 1) // 2]
        return bufs[2].at[(dy + 1) + (dx + 1) // 2]

    def out(self, dy, dx):
        return self.slot((self.rows[0], self.cols[0], self.corners[0]), dy, dx)

    def inc(self, dy, dx):
        return self.slot((self.rows[1], self.cols[1], self.corners[1]), dy, dx)

    def copy(self, dy, dx):
        i = DIRS.index((dy, dx))
        return remote(self.out(dy, dx), self.inc(dy, dx), self.send.at[i], self.recv.at[i], self.place.neighbour(dy, dx))


ORDER = [(0, 1), (0, -1), (1, 0), (-1, 0), (1, 1), (1, -1), (-1, 1), (-1, -1)]


def pack_halo(e, core):
    for dy, dx in ORDER:
        r0, r1 = {-1: (0, 64), 0: (0, 256), 1: (192, 256)}[dy]
        if dx == 0:
            for t in range(2):
                e.out(dy, dx)[:, t] = core(t, r0, r1)
        else:
            e.out(dy, dx)[...] = pack(core((dx + 1) // 2, r0, r1), dx)


def unpack_halo(e, ext):
    for dy, dx in ORDER:
        e.copy(dy, dx).wait_recv()
    for dy in (-1, 1):
        r0 = 320 if dy < 0 else 0
        for t in range(2):
            ext[:, t, r0 : r0 + 64] = e.inc(dy, 0)[:, t]
    for dy in (-1, 0, 1):
        r0, r1 = {-1: (320, 384), 0: (64, 320), 1: (0, 64)}[dy]
        left, right = unpack(e.inc(dy, -1)[...], -1), unpack(e.inc(dy, 1)[...], 1)
        ext[:, 2, r0:r1] = jnp.where(half_lanes(left.shape), left, right)


def pack_fold(e, g):
    for dy, dx in ORDER:
        r0, r1 = {-1: (0, 64), 0: (64, 320), 1: (320, 384)}[dy]
        if dx == 0:
            for t in range(2):
                e.out(dy, dx)[:, t] = g[:, t, r0:r1]
        else:
            e.out(dy, dx)[...] = pack(g[:, 2, r0:r1], -dx)


def fold(e, g, total):
    for dy, dx in ORDER:
        e.copy(dy, dx).wait_recv()
    for t in range(2):
        total[:, t] = g[:, t, 64:320]
    for dy, dx in ORDER:
        r0, r1 = {-1: (192, 256), 0: (0, 256), 1: (0, 64)}[dy]
        if dx == 0:
            for t in range(2):
                total[:, t, r0:r1] += e.inc(dy, dx)[:, t]
        else:
            t = (1 - dx) // 2
            total[:, t, r0:r1] += keep_side(unpack(e.inc(dy, dx)[...], -dx), -dx)


def start_all(e):
    for dy, dx in ORDER:
        e.copy(dy, dx).start()


def wait_sent(e):
    for dy, dx in ORDER:
        e.copy(dy, dx).wait_send()


class Summer:
    def __init__(self, place, gp, pair, ready, plane, cross, whole, sems):
        self.p, self.gp, self.pair, self.ready, self.pl = place, gp, pair, ready, plane
        self.cross, self.whole, self.sems = cross, whole, sems

    def pair_copy(self, j):
        return remote(self.gp.at[1 - self.p.core, j], self.pair.at[j], self.sems[0].at[j], self.sems[1].at[j], self.p.sibling())

    def plane_copy(self, k):
        j, device = self.p.plane(k)
        return j, remote(self.ready.at[j], self.pl.at[k], self.sems[2].at[k], self.sems[3].at[k], device)

    def cross_copy(self, k):
        x, device = self.p.column(k)
        return remote(self.cross.at[self.p.x], self.cross.at[self.p.x], self.sems[4].at[k], self.sems[5].at[k], device)

    def cross_wait(self, k):
        self.cross_copy(k).wait_recv()

    def spread_copy(self, k):
        j, device = self.p.plane(k)
        own = self.whole.at[self.p.core, self.p.spot]
        return remote(own, own, self.sems[6].at[k], self.sems[7].at[k], device)

    def forward_copy(self, k):
        j, _ = self.p.plane(self.back(k))
        own = self.whole.at[self.p.core, j]
        return remote(own, own, self.sems[8].at[k], self.sems[9].at[k], self.p.sibling())

    def back(self, k):
        return lax.rem(4 - k // 4, 4) * 4 + lax.rem(4 - lax.rem(k, 4), 4)

    def begin(self):
        lax.fori_loop(0, 16, lambda k, c: (self.pair_copy(self.p.plane(k)[0]).start(), c)[1], 0)

    def scatter(self):
        def step(k, c):
            j, copy = self.plane_copy(k)
            self.pair_copy(j).wait_recv()
            self.ready[j] = self.gp[self.p.core, j] + self.pair[j]
            copy.start()
            return c

        lax.fori_loop(1, 16, step, 0)
        me = self.p.spot
        self.pair_copy(me).wait_recv()
        self.ready[me] = self.gp[self.p.core, me] + self.pair[me]

    def across(self):
        total = self.ready[self.p.spot]

        def step(k, c):
            self.plane_copy(k)[1].wait_recv()
            return c + self.pl[k]

        total = lax.fori_loop(1, 16, step, total)
        self.cross[self.p.x] = total
        lax.fori_loop(1, 4, lambda k, c: (self.cross_copy(k).start(), c)[1], 0)

    def spread(self):
        lax.fori_loop(1, 4, lambda k, c: (self.cross_copy(k).wait_recv(), c)[1], 0)
        self.whole[self.p.core, self.p.spot] = (self.cross[0] + self.cross[1]) + (self.cross[2] + self.cross[3])
        lax.fori_loop(1, 16, lambda k, c: (self.spread_copy(k).start(), c)[1], 0)
        self.forward_copy(0).start()

    def forward(self):
        def step(k, c):
            self.spread_copy(k).wait_recv()
            self.forward_copy(k).start()
            return c

        lax.fori_loop(1, 16, step, 0)

    def finish(self):
        lax.fori_loop(0, 16, lambda k, c: (self.forward_copy(k).wait_recv(), c)[1], 0)

    def sent(self):
        def step(k, c):
            self.pair_copy(self.p.plane(k)[0]).wait_send()
            self.forward_copy(k).wait_send()
            return c

        lax.fori_loop(0, 16, step, 0)

        def more(k, c):
            self.plane_copy(k)[1].wait_send()
            self.spread_copy(k).wait_send()
            return c

        lax.fori_loop(1, 16, more, 0)
        lax.fori_loop(1, 4, lambda k, c: (self.cross_copy(k).wait_send(), c)[1], 0)


def greet(p, summing):
    barrier = pltpu.get_barrier_semaphore()

    def hello(device):
        pl.semaphore_signal(barrier, inc=1, device_id=device, device_id_type=MESH)

    for dy, dx in DIRS:
        hello(p.neighbour(dy, dx))
    count = 8
    if summing:
        hello(p.sibling())
        lax.fori_loop(1, 16, lambda k, c: (hello(p.plane(k)[1]), c)[1], 0)
        lax.fori_loop(1, 4, lambda k, c: (hello(p.column(k)[1]), c)[1], 0)
        count += 19
    return lambda: pl.semaphore_wait(barrier, count)


def edge_scratch():
    return [
        pltpu.VMEM((2, 2, 4, 2, 64, 128), f32),
        pltpu.VMEM((2, 2, 4, 128, 128), f32),
        pltpu.VMEM((2, 4, 4, 32, 128), f32),
        pltpu.SemaphoreType.DMA((2, 8)),
    ]


def make_edges(p, rows, cols, corners, sems):
    pair = lambda ref: (ref.at[0], ref.at[1])
    return Edges(p, pair(rows), pair(cols), pair(corners), pair(sems))


def sum_scratch():
    return [
        pltpu.VMEM((16, 32, 128), f32),
        pltpu.VMEM((16, 32, 128), f32),
        pltpu.VMEM((16, 32, 128), f32),
        pltpu.VMEM((4, 32, 128), f32),
        pltpu.VMEM((2, 16, 32, 128), f32),
        pltpu.SemaphoreType.DMA((10, 16)),
    ]


def halo_kernel(obj, ext, rows, cols, corners, sems):
    p = Place()
    ready = greet(p, False)
    e = make_edges(p, rows, cols, corners, sems)
    core = lambda t, r0, r1: obj[:, r0:r1, t * 128 : t * 128 + 128]
    pack_halo(e, core)
    ready()
    start_all(e)
    for t in range(2):
        ext[:, t, 64:320] = core(t, 0, 256)
    unpack_halo(e, ext)
    wait_sent(e)


def step_size(probe):
    power = probe[0] * probe[0] + probe[1] * probe[1]
    peak = jnp.max(power, axis=(0, 1), keepdims=True) + 1e-06
    return object_rate / peak


def probe_update(probe, whole, out):
    for h in range(2):
        for t in range(2):
            cols = slice(t * 128, t * 128 + 128)
            grad = whole[h, 8 * t : 8 * t + 8].reshape(256, 128)
            out[h, :, cols] = probe[h, :, cols] - (probe_rate / (NTY * NTX)) * grad


def step_kernel(last, g, gp, old, probe, *refs):
    obj_out, probe_out, total = refs[:3]
    p = Place()
    ready = greet(p, True)
    f = make_edges(p, *refs[3:7])
    s = Summer(p, gp, *refs[7:12], [refs[12].at[i] for i in range(10)])
    pack_fold(f, g)
    ready()
    start_all(f)
    s.begin()
    s.scatter()
    rate = step_size(probe)
    fold(f, g, total)
    if last:
        for t in range(2):
            obj_out[:, :, t * 128 : t * 128 + 128] = old[:, t, 64:320] - rate * total[:, t]
    else:
        for t in range(2):
            obj_out[:, t, 64:320] = old[:, t, 64:320] - rate * total[:, t]
        e = make_edges(p, *refs[13:17])
        pack_halo(e, lambda t, r0, r1: obj_out[:, t, 64 + r0 : 64 + r1])
        start_all(e)
    s.across()
    s.spread()
    s.forward()
    if not last:
        unpack_halo(e, obj_out)
    s.finish()
    probe_update(probe, s.whole, probe_out)
    wait_sent(f)
    s.sent()
    if not last:
        wait_sent(e)


def halo(obj):
    return pl.pallas_call(
        halo_kernel,
        out_shape=jax.ShapeDtypeStruct((4, 3, 384, 128), f32),
        in_specs=[V],
        out_specs=V,
        scratch_shapes=edge_scratch(),
        compiler_params=pltpu.CompilerParams(collective_id=0, has_side_effects=True, vmem_limit_bytes=40 << 20),
        name="halo",
    )(obj)


def step(last, g, gp, old, probe):
    obj_shape = (4, 256, 256) if last else (4, 3, 384, 128)
    scratch = [pltpu.VMEM((4, 2, 256, 128), f32)] + edge_scratch() + sum_scratch()
    if not last:
        scratch += edge_scratch()
    return pl.pallas_call(
        functools.partial(step_kernel, last),
        out_shape=(jax.ShapeDtypeStruct(obj_shape, f32), jax.ShapeDtypeStruct((2, 256, 256), f32)),
        in_specs=[V] * 4,
        out_specs=(V, V),
        scratch_shapes=scratch,
        compiler_params=pltpu.CompilerParams(
            collective_id=2 if last else 1, has_side_effects=True, vmem_limit_bytes=48 << 20
        ),
        name="final_step" if last else "middle_step",
    )(g, gp.reshape(2, 16, 32, 128), old, probe)


def body(object_slices, probe, position_count, offsets, intensities):
    tab = jnp.asarray(tables())
    count, off = position_count[0], offsets[0, 0]
    inten = intensities[0, 0]
    ext = halo(object_slices.reshape(4, 256, 256))
    g, gp = compute(count, off, ext, probe, inten, tab)
    ext, probe = step(False, g, gp, ext, probe)
    g, gp = compute(count, off, ext, probe, inten, tab)
    core, probe = step(True, g, gp, ext, probe)
    return core.reshape(2, 2, 256, 256), probe


def solution(mesh):
    placed = (
        P(None, None, "ty", "tx"),
        P(),
        P("ty", "tx"),
        P("ty", "tx", None, None),
        P("ty", "tx", None, None, None),
    )
    return jax.shard_map(
        body,
        mesh=mesh,
        in_specs=placed,
        out_specs=(P(None, None, "ty", "tx"), P()),
        check_vma=False,
    )
```

time: 1070 us -> 171 us (0.16); the launches traced: 1060 us -> 171 us
  waiting for transfers between devices: 426 us -> 0 us
  matrix products: 280 us -> 0 us
  Pallas kernels: 0 us -> 164 us
  local copies, waits for them, and re-layouts: 162 us -> 5.39 us
  loops' own time: 96.4 us -> 0 us
  other arithmetic: 46.5 us -> 0 us
  starting transfers between devices: 30 us -> 0 us
  between operations: 15.9 us -> 1.56 us
    dot_general x260 -> x0, matrix products: 280 us -> none  [matmul(): jnp.dot(left, right, precision=lax.Precision.HIGHEST, preferred_element_t...]
    psum x2 -> x0, waiting for transfers between devices: 273 us -> none  [body(): summed = lax.psum(probe_grad, ('ty', 'tx'))]
    pallas_call x0 -> x5, Pallas kernels: none -> 164 us  [the longest x2 111 us: step(): pl.pallas_call(functools.partial(step_kernel, last), out_shape=(jax.Shape...]
    ppermute x16 -> x0, waiting for transfers between devices: 153 us -> none  [the longest x8 125 us: extended_2(): lax.ppermute(lax.slice_in_dim(block, 0, width, axis=dim), axis, backward)]
    another operation x2 -> x0, loops' own time: 96.4 us -> none  [body(): grads, probe_grad = lax.fori_loop(zero, count, visit, start)]
    dynamic_update_slice x8 -> x0, local copies, waits for them, and re-layouts: 90.6 us -> none  [visit(): lax.dynamic_update_slice(local, current + object_part, (zero, top, left))]
    ppermute x16 -> x0, starting transfers between devices: 29.9 us -> none  [the longest x8 18.6 us: extended_2(): lax.ppermute(lax.slice_in_dim(block, 0, width, axis=dim), axis, backward)]
    while x66 -> x0, local copies, waits for them, and re-layouts: 28.6 us -> none
  transfers between devices with their start and end apart: 18 -> 0, of which waited for: 13 -> 0; matrix products, arithmetic and copies ran while one was open for 2% -> 0% of each run, Pallas kernels for 0% -> 0%
where the time goes in v1:
time: 171 us
  Pallas kernels  164 us (96%)
  local copies, waits for them, and re-layouts  5.39 us (3%)
    pallas_call x2, Pallas kernels, step(): pl.pallas_call(functools.partial(step_kernel, last), out_shape=(jax.Shape...  111 us
    pallas_call x2, Pallas kernels, compute(): pl.pallas_call(compute_kernel, out_shape=(jax.ShapeDtypeStruct((4, 3, 384...  30.7 us
    pallas_call x1, Pallas kernels, halo(): pl.pallas_call(halo_kernel, out_shape=jax.ShapeDtypeStruct((4, 3, 384, 12...  21.9 us
    unnamed x16, local copies, waits for them, and re-layouts  4.41 us

profile of v1, /device:TPU:1, one launch (start us, length us, event | category | flops | bytes accessed | tf_op | source)
XLA Modules:
  0.0 170.8 jit_solution(13984627723907311793)
XLA Ops:
  0.6 0.0 copy-start.2
  0.6 0.0 copy-start.5
  0.7 0.0 copy-start.3
  1.5 1.0 copy.9.off_ref
  2.4 0.0 copy-start.6
  2.4 1.2 copy-done.6
  3.7 21.9 %halo.1.ext_ref.old = f32[4,3,384,128]{3,2,1,0:T(8,128)S(1)} custom-call(f32[4,256,256]{2,1,0:T(8,128)S(1)} %bitcast.11), custom_call_target="tpu_custom_call" | custom-call | tf_op jit(solution)/shard_map/halo/pallas_call | solution.py:470
  25.5 0.0 copy-done.2
  25.6 0.0 copy-done.5
  25.6 0.0 copy-done.3
  25.6 0.0 copy-start
  25.6 15.3 %positions.2 = (f32[4,3,384,128]{3,2,1,0:T(8,128)S(1)}, f32[2,2,256,128]{3,2,1,0:T(8,128)S(1)}) custom-call(s32[1]{0:T(128)} %bitcast.7.count_ref, s32[5,2]{1,0:T(8,128)S(1)} %copy.9.off_ref, f32[4,3,384,128]{3,2,1,0:T(8,128)S(1)} %halo.1.ext_ref.old, f32[2,256,256]{2,1,0:T(8,128)S(1)} %copy-done.5, f32[5,256,256]{2,1,0:T(8,128)S(1)} %bitcast.9, ...), custom_call_target="tpu_custom_call" | custom-call | tf_op jit(solution)/shard_map/positions/pallas_call | solution.py:116
  40.9 0.0 copy-done
  41.0 0.0 copy-start.4
  41.0 1.4 copy-done.4
  42.4 64.3 %middle_step.1 = (f32[4,3,384,128]{3,2,1,0:T(8,128)S(1)}, f32[2,256,256]{2,1,0:T(8,128)S(1)}) custom-call(f32[4,3,384,128]{3,2,1,0:T(8,128)} %copy-done.4, f32[2,16,32,128]{3,2,1,0:T(8,128)S(1)} %bitcast.14, f32[4,3,384,128]{3,2,1,0:T(8,128)} %copy-done, f32[2,256,256]{2,1,0:T(8,128)S(1)} %copy-done.5), custom_call_target="tpu_custom_call" | custom-call | tf_op jit(solution)/shard_map/middle_step/pallas_call | solution.py:486
  106.7 0.0 copy-start.1
  106.7 15.4 %positions.3 = (f32[4,3,384,128]{3,2,1,0:T(8,128)S(1)}, f32[2,2,256,128]{3,2,1,0:T(8,128)S(1)}) custom-call(s32[1]{0:T(128)} %bitcast.8.count_ref, s32[5,2]{1,0:T(8,128)S(1)} %copy.9.off_ref, f32[4,3,384,128]{3,2,1,0:T(8,128)S(1)} %get-tuple-element.12.ext_ref.old, f32[2,256,256]{2,1,0:T(8,128)S(1)} %get-tuple-element.13.probe_ref.probe, ...), custom_call_target="tpu_custom_call" | custom-call | tf_op jit(solution)/shard_map/positions/pallas_call | solution.py:116
  122.0 0.0 copy-done.1
  122.0 47.0 %final_step.1 = (f32[4,256,256]{2,1,0:T(8,128)S(1)}, f32[2,256,256]{2,1,0:T(8,128)S(1)}) custom-call(f32[4,3,384,128]{3,2,1,0:T(8,128)S(1)} %get-tuple-element.14.g, f32[2,16,32,128]{3,2,1,0:T(8,128)S(1)} %bitcast.13, f32[4,3,384,128]{3,2,1,0:T(8,128)} %copy-done.1, f32[2,256,256]{2,1,0:T(8,128)S(1)} %get-tuple-element.13.probe_ref.probe), custom_call_target="tpu_custom_call" | custom-call | tf_op jit(solution)/shard_map/final_step/pallas_call | solution.py:486
  169.0 1.0 copy.13
  170.0 0.8 copy.14
Async XLA Ops:
  0.6 24.9 %copy-start.2 = (bf16[2,3,2,256,256]{4,3,2,1,0:T(8,128)(2,1)S(1)}, bf16[2,3,2,256,256]{4,3,2,1,0:T(8,128)(2,1)}, u32[]{:S(2)}) copy-start(bf16[2,3,2,256,256]{4,3,2,1,0:T(8,128)(2,1)} %constant.2.clone.tab) | copy-start | bytes 4718596
  0.6 24.9 %copy-start.5 = (f32[2,256,256]{2,1,0:T(8,128)S(1)}, f32[2,256,256]{2,1,0:T(8,128)}, u32[]{:S(2)}) copy-start(f32[2,256,256]{2,1,0:T(8,128)} %probe.1) | copy-start | bytes 1572868
  0.7 24.9 %copy-start.3 = (f32[1,1,5,256,256]{4,3,2,1,0:T(8,128)S(1)}, f32[1,1,5,256,256]{4,3,2,1,0:T(8,128)}, u32[]{:S(2)}) copy-start(f32[1,1,5,256,256]{4,3,2,1,0:T(8,128)} %param.10) | copy-start | bytes 3932164
  2.4 1.2 copy-start.6
  25.6 15.4 %copy-start = (f32[4,3,384,128]{3,2,1,0:T(8,128)}, f32[4,3,384,128]{3,2,1,0:T(8,128)S(1)}, u32[]{:S(2)}) copy-start(f32[4,3,384,128]{3,2,1,0:T(8,128)S(1)} %halo.1.ext_ref.old) | copy-start | bytes 7077892
  41.0 1.4 copy-start.4
  106.7 15.4 %copy-start.1 = (f32[4,3,384,128]{3,2,1,0:T(8,128)}, f32[4,3,384,128]{3,2,1,0:T(8,128)S(1)}, u32[]{:S(2)}) copy-start(f32[4,3,384,128]{3,2,1,0:T(8,128)S(1)} %get-tuple-element.12.ext_ref.old) | copy-start | bytes 7077892

commit v2 on v1

--- a/solution.py
+++ b/solution.py
@@ -66,64 +66,6 @@
     return shared - right(tab, which, 2, imag), shared + right(tab, which, 1, real)
 
 
-def compute_kernel(count_ref, off_ref, ext_ref, probe_ref, int_ref, tab, g_ref, gp_ref, win, moved, mid):
-    g_ref[...] = jnp.zeros_like(g_ref)
-    gp_ref[...] = jnp.zeros_like(gp_ref)
-    lane = lax.broadcasted_iota(jnp.int32, (256, 128), 1)
-
-    def visit(s, carry):
-        top, left_col = off_ref[s, 0], off_ref[s, 1]
-        inner = left_col >= 64
-        t0 = jnp.where(inner, 0, 2)
-        t1 = jnp.where(inner, 1, 0)
-        t2 = jnp.where(inner, 2, 1)
-        shift = jnp.where(inner, left_col - 64, left_col + 64)
-        keep = lane < 128 - shift
-        rows = pl.ds(top, 256)
-        for p in range(4):
-            a, b, c = [pltpu.roll(ext_ref[p, t, rows, :], 128 - shift, 1) for t in (t0, t1, t2)]
-            win[p, :, 0:128] = jnp.where(keep, a, b)
-            win[p, :, 128:256] = jnp.where(keep, b, c)
-        pr, pi = probe_ref[0], probe_ref[1]
-        moved[0], moved[1] = sandwich(tab, 1, pr * win[0] - pi * win[1], pr * win[1] + pi * win[0], mid)
-        er = moved[0] * win[2] - moved[1] * win[3]
-        ei = moved[0] * win[3] + moved[1] * win[2]
-        fr, fi = sandwich(tab, 0, er, ei, mid)
-        misfit = fr * fr + fi * fi - int_ref[s]
-        cr, ci = sandwich(tab, 0, misfit * fr, -(misfit * fi), mid)
-        g2r = moved[0] * cr - moved[1] * ci
-        g2i = -(moved[0] * ci + moved[1] * cr)
-        wr, wi = sandwich(tab, 1, win[2] * cr - win[3] * ci, win[2] * ci + win[3] * cr, mid)
-        g1r = probe_ref[0] * wr - probe_ref[1] * wi
-        g1i = -(probe_ref[0] * wi + probe_ref[1] * wr)
-        for h, gp in enumerate((win[0] * wr - win[1] * wi, -(win[0] * wi + win[1] * wr))):
-            gp_ref[h, 0] += gp[:, 0:128]
-            gp_ref[h, 1] += gp[:, 128:256]
-        before = lane < shift
-        for p, g in enumerate((g1r, g1i, g2r, g2i)):
-            a, b = pltpu.roll(g[:, 0:128], shift, 1), pltpu.roll(g[:, 128:256], shift, 1)
-            g_ref[p, t0, rows, :] += jnp.where(before, 0.0, a)
-            g_ref[p, t1, rows, :] += jnp.where(before, a, b)
-            g_ref[p, t2, rows, :] += jnp.where(before, b, 0.0)
-        return carry
-
-    lax.fori_loop(0, count_ref[0], visit, 0)
-
-
-def compute(count, off, ext, probe, inten, tab):
-    vmem = pl.BlockSpec(memory_space=pltpu.VMEM)
-    smem = pl.BlockSpec(memory_space=pltpu.SMEM)
-    return pl.pallas_call(
-        compute_kernel,
-        out_shape=(jax.ShapeDtypeStruct((4, 3, 384, 128), f32), jax.ShapeDtypeStruct((2, 2, 256, 128), f32)),
-        in_specs=[smem, smem, vmem, vmem, vmem, vmem],
-        out_specs=(vmem, vmem),
-        scratch_shapes=[pltpu.VMEM((4, 256, 256), f32), pltpu.VMEM((2, 256, 256), f32), pltpu.VMEM((2, 256, 256), f32)],
-        compiler_params=pltpu.CompilerParams(vmem_limit_bytes=40 << 20),
-        name="positions",
-    )(count, off, ext, probe, inten, tab)
-
-
 NTY, NTX = 8, 16
 MESH = pl.DeviceIdType.MESH
 DIRS = [(dy, dx) for dy in (-1, 0, 1) for dx in (-1, 0, 1) if (dy, dx) != (0, 0)]
@@ -378,43 +320,163 @@
     return lambda: pl.semaphore_wait(barrier, count)
 
 
-def edge_scratch():
-    return [
-        pltpu.VMEM((2, 2, 4, 2, 64, 128), f32),
-        pltpu.VMEM((2, 2, 4, 128, 128), f32),
-        pltpu.VMEM((2, 4, 4, 32, 128), f32),
-        pltpu.SemaphoreType.DMA((2, 8)),
-    ]
-
-
-def make_edges(p, rows, cols, corners, sems):
+EXCHANGES = 8
+SUMS = ITERS
+
+
+def exchange(p, refs, i):
+    rows, cols, corners, sems = [ref.at[i] for ref in refs]
     pair = lambda ref: (ref.at[0], ref.at[1])
     return Edges(p, pair(rows), pair(cols), pair(corners), pair(sems))
 
 
-def sum_scratch():
-    return [
-        pltpu.VMEM((16, 32, 128), f32),
-        pltpu.VMEM((16, 32, 128), f32),
-        pltpu.VMEM((16, 32, 128), f32),
-        pltpu.VMEM((4, 32, 128), f32),
-        pltpu.VMEM((2, 16, 32, 128), f32),
-        pltpu.SemaphoreType.DMA((10, 16)),
-    ]
-
-
-def halo_kernel(obj, ext, rows, cols, corners, sems):
+def shifts(off_ref, s):
+    top, left_col = off_ref[s, 0], off_ref[s, 1]
+    inner = left_col >= 64
+    first = jnp.where(inner, 0, 2)
+    second = jnp.where(inner, 1, 0)
+    third = jnp.where(inner, 2, 1)
+    return top, jnp.where(inner, left_col - 64, left_col + 64), (first, second, third)
+
+
+def take_window(off_ref, s, ext, win):
+    top, shift, tiles = shifts(off_ref, s)
+    keep = lax.broadcasted_iota(jnp.int32, (256, 128), 1) < 128 - shift
+    for p in range(2):
+        a, b, c = [pltpu.roll(ext[p, t, pl.ds(top, 256), :], 128 - shift, 1) for t in tiles]
+        win[s, p, :, 0:128] = jnp.where(keep, a, b)
+        win[s, p, :, 128:256] = jnp.where(keep, b, c)
+
+
+def add_window(off_ref, count_ref, s, pair, slide, acc):
+    top, shift, (first, second, third) = shifts(off_ref, s)
+    lane = lax.broadcasted_iota(jnp.int32, (256, 128), 1)
+    before = lane < shift
+    active = lane * 0 + s < count_ref[0]
+    for p in range(2):
+        a, b = [
+            pltpu.roll(jnp.where(active, pair[p][:, t * 128 : t * 128 + 128], 0.0), shift, 1) for t in range(2)
+        ]
+        slide[p, 0, 128:384] = jnp.where(before, 0.0, a)
+        slide[p, 1, 128:384] = jnp.where(before, a, b)
+        slide[p, 2, 128:384] = jnp.where(before, b, 0.0)
+    inner = first == 0
+    source = (jnp.where(inner, 0, 1), jnp.where(inner, 1, 2), jnp.where(inner, 2, 0))
+    for p in range(2):
+        for t in range(3):
+            acc[p, t] += slide[p, source[t], pl.ds(128 - top, 384), :]
+
+
+def program_kernel(
+    count_ref, off_ref, obj, probe_in, inten_hbm, tab_hbm, obj_out, probe_out,
+    tab, inten, ext1, ext2, acc1, acc2, gp, slide, win1, win2, moved, back, mid, total, probe,
+    rows, cols, corners, edge_sems, pair, made, plane, cross, whole, sum_sems, local_sems,
+):
     p = Place()
-    ready = greet(p, False)
-    e = make_edges(p, rows, cols, corners, sems)
-    core = lambda t, r0, r1: obj[:, r0:r1, t * 128 : t * 128 + 128]
-    pack_halo(e, core)
+    ready = greet(p, True)
+    edges = (rows, cols, corners, edge_sems)
+    tab_copy = pltpu.make_async_copy(tab_hbm, tab, local_sems.at[0])
+    inten_copy = pltpu.make_async_copy(inten_hbm, inten, local_sems.at[1])
+    tab_copy.start()
+    inten_copy.start()
+    halo1, halo2 = exchange(p, edges, 0), exchange(p, edges, 1)
+    for k, e in enumerate((halo1, halo2)):
+        pack_halo(e, lambda t, r0, r1: obj[2 * k : 2 * k + 2, r0:r1, t * 128 : t * 128 + 128])
     ready()
-    start_all(e)
+    start_all(halo1)
+    start_all(halo2)
     for t in range(2):
-        ext[:, t, 64:320] = core(t, 0, 256)
-    unpack_halo(e, ext)
-    wait_sent(e)
+        ext1[:, t, 64:320] = obj[0:2, :, t * 128 : t * 128 + 128]
+        ext2[:, t, 64:320] = obj[2:4, :, t * 128 : t * 128 + 128]
+    slide[...] = jnp.zeros_like(slide)
+    probe[...] = probe_in[...]
+    tab_copy.wait()
+    inten_copy.wait()
+    unpack_halo(halo1, ext1)
+
+    for it in range(ITERS):
+        last = it == ITERS - 1
+        acc1[...] = jnp.zeros_like(acc1)
+        acc2[...] = jnp.zeros_like(acc2)
+        gp[...] = jnp.zeros_like(gp)
+
+        def forward(s, carry):
+            take_window(off_ref, s, ext1, win1)
+            pr, pi, wr, wi = probe[0], probe[1], win1[s, 0], win1[s, 1]
+            moved[s, 0], moved[s, 1] = sandwich(tab, 1, pr * wr - pi * wi, pr * wi + pi * wr, mid)
+            return carry
+
+        lax.fori_loop(0, MAXPOS, forward, 0)
+        unpack_halo(halo2, ext2)
+
+        def detector(s, carry):
+            take_window(off_ref, s, ext2, win2)
+            er = moved[s, 0] * win2[s, 0] - moved[s, 1] * win2[s, 1]
+            ei = moved[s, 0] * win2[s, 1] + moved[s, 1] * win2[s, 0]
+            fr, fi = sandwich(tab, 0, er, ei, mid)
+            misfit = fr * fr + fi * fi - inten[s]
+            cr, ci = sandwich(tab, 0, misfit * fr, -(misfit * fi), mid)
+            back[s, 0] = win2[s, 0] * cr - win2[s, 1] * ci
+            back[s, 1] = win2[s, 0] * ci + win2[s, 1] * cr
+            g2 = (moved[s, 0] * cr - moved[s, 1] * ci, -(moved[s, 0] * ci + moved[s, 1] * cr))
+            add_window(off_ref, count_ref, s, g2, slide, acc2)
+            return carry
+
+        lax.fori_loop(0, MAXPOS, detector, 0)
+        fold2 = exchange(p, edges, 4 * it + 2)
+        pack_fold(fold2, acc2)
+        start_all(fold2)
+
+        def adjoint(s, carry):
+            wr, wi = sandwich(tab, 1, back[s, 0], back[s, 1], mid)
+            g1 = (probe[0] * wr - probe[1] * wi, -(probe[0] * wi + probe[1] * wr))
+            add_window(off_ref, count_ref, s, g1, slide, acc1)
+            active = lax.broadcasted_iota(jnp.int32, (256, 128), 1) * 0 + s < count_ref[0]
+            parts = (win1[s, 0] * wr - win1[s, 1] * wi, -(win1[s, 0] * wi + win1[s, 1] * wr))
+            for h in range(2):
+                for t in range(2):
+                    part = jnp.where(active, parts[h][:, t * 128 : t * 128 + 128], 0.0)
+                    gp[h, 8 * t : 8 * t + 8] += part.reshape(8, 32, 128)
+            return carry
+
+        lax.fori_loop(0, MAXPOS, adjoint, 0)
+        s = Summer(p, gp, *[ref.at[it] for ref in (pair, made, plane, cross, whole)], [sum_sems.at[it, i] for i in range(10)])
+        s.begin()
+        fold1 = exchange(p, edges, 4 * it + 3)
+        pack_fold(fold1, acc1)
+        start_all(fold1)
+        s.scatter()
+        rate = step_size(probe)
+        fold(fold2, acc2, total)
+        if last:
+            for t in range(2):
+                obj_out[2:4, :, t * 128 : t * 128 + 128] = ext2[:, t, 64:320] - rate * total[:, t]
+        else:
+            for t in range(2):
+                ext2[:, t, 64:320] -= rate * total[:, t]
+        s.across()
+        fold(fold1, acc1, total)
+        if last:
+            for t in range(2):
+                obj_out[0:2, :, t * 128 : t * 128 + 128] = ext1[:, t, 64:320] - rate * total[:, t]
+            s.spread()
+        else:
+            for t in range(2):
+                ext1[:, t, 64:320] -= rate * total[:, t]
+            halo1, halo2 = exchange(p, edges, 4), exchange(p, edges, 5)
+            pack_halo(halo1, lambda t, r0, r1: ext1[:, t, 64 + r0 : 64 + r1])
+            start_all(halo1)
+            s.spread()
+            pack_halo(halo2, lambda t, r0, r1: ext2[:, t, 64 + r0 : 64 + r1])
+            start_all(halo2)
+        s.forward()
+        if not last:
+            unpack_halo(halo1, ext1)
+        s.finish()
+        probe_update(probe, s.whole, probe_out if last else probe)
+        s.sent()
+    for i in range(EXCHANGES):
+        wait_sent(exchange(p, edges, i))
 
 
 def step_size(probe):
@@ -431,81 +493,59 @@
             out[h, :, cols] = probe[h, :, cols] - (probe_rate / (NTY * NTX)) * grad
 
 
-def step_kernel(last, g, gp, old, probe, *refs):
-    obj_out, probe_out, total = refs[:3]
-    p = Place()
-    ready = greet(p, True)
-    f = make_edges(p, *refs[3:7])
-    s = Summer(p, gp, *refs[7:12], [refs[12].at[i] for i in range(10)])
-    pack_fold(f, g)
-    ready()
-    start_all(f)
-    s.begin()
-    s.scatter()
-    rate = step_size(probe)
-    fold(f, g, total)
-    if last:
-        for t in range(2):
-            obj_out[:, :, t * 128 : t * 128 + 128] = old[:, t, 64:320] - rate * total[:, t]
-    else:
-        for t in range(2):
-            obj_out[:, t, 64:320] = old[:, t, 64:320] - rate * total[:, t]
-        e = make_edges(p, *refs[13:17])
-        pack_halo(e, lambda t, r0, r1: obj_out[:, t, 64 + r0 : 64 + r1])
-        start_all(e)
-    s.across()
-    s.spread()
-    s.forward()
-    if not last:
-        unpack_halo(e, obj_out)
-    s.finish()
-    probe_update(probe, s.whole, probe_out)
-    wait_sent(f)
-    s.sent()
-    if not last:
-        wait_sent(e)
-
-
-def halo(obj):
+def run(count, off, obj, probe, inten, tab):
+    smem = pl.BlockSpec(memory_space=pltpu.SMEM)
+    anywhere = pl.BlockSpec(memory_space=pl.ANY)
+    vm = pltpu.VMEM
+    slots = vm((MAXPOS, 2, 256, 256), f32)
     return pl.pallas_call(
-        halo_kernel,
-        out_shape=jax.ShapeDtypeStruct((4, 3, 384, 128), f32),
-        in_specs=[V],
-        out_specs=V,
-        scratch_shapes=edge_scratch(),
-        compiler_params=pltpu.CompilerParams(collective_id=0, has_side_effects=True, vmem_limit_bytes=40 << 20),
-        name="halo",
-    )(obj)
-
-
-def step(last, g, gp, old, probe):
-    obj_shape = (4, 256, 256) if last else (4, 3, 384, 128)
-    scratch = [pltpu.VMEM((4, 2, 256, 128), f32)] + edge_scratch() + sum_scratch()
-    if not last:
-        scratch += edge_scratch()
-    return pl.pallas_call(
-        functools.partial(step_kernel, last),
-        out_shape=(jax.ShapeDtypeStruct(obj_shape, f32), jax.ShapeDtypeStruct((2, 256, 256), f32)),
-        in_specs=[V] * 4,
+        program_kernel,
+        out_shape=(jax.ShapeDtypeStruct((4, 256, 256), f32), jax.ShapeDtypeStruct((2, 256, 256), f32)),
+        in_specs=[smem, smem, V, V, anywhere, anywhere],
         out_specs=(V, V),
-        scratch_shapes=scratch,
-        compiler_params=pltpu.CompilerParams(
-            collective_id=2 if last else 1, has_side_effects=True, vmem_limit_bytes=48 << 20
-        ),
-        name="final_step" if last else "middle_step",
-    )(g, gp.reshape(2, 16, 32, 128), old, probe)
+        scratch_shapes=[
+            vm((2, 3, 2, 256, 256), bf),
+            vm((MAXPOS, 256, 256), f32),
+            vm((2, 3, 384, 128), f32),
+            vm((2, 3, 384, 128), f32),
+            vm((2, 3, 384, 128), f32),
+            vm((2, 3, 384, 128), f32),
+            vm((2, 16, 32, 128), f32),
+            vm((2, 3, 512, 128), f32),
+            slots,
+            slots,
+            slots,
+            slots,
+            vm((2, 256, 256), f32),
+            vm((2, 2, 256, 128), f32),
+            vm((2, 256, 256), f32),
+            vm((EXCHANGES, 2, 2, 2, 2, 64, 128), f32),
+            vm((EXCHANGES, 2, 2, 2, 128, 128), f32),
+            vm((EXCHANGES, 2, 4, 2, 32, 128), f32),
+            pltpu.SemaphoreType.DMA((EXCHANGES, 2, 8)),
+            vm((SUMS, 16, 32, 128), f32),
+            vm((SUMS, 16, 32, 128), f32),
+            vm((SUMS, 16, 32, 128), f32),
+            vm((SUMS, 4, 32, 128), f32),
+            vm((SUMS, 2, 16, 32, 128), f32),
+            pltpu.SemaphoreType.DMA((SUMS, 10, 16)),
+            pltpu.SemaphoreType.DMA((2,)),
+        ],
+        compiler_params=pltpu.CompilerParams(collective_id=0, has_side_effects=True, vmem_limit_bytes=58 << 20),
+        name="iterations",
+    )(count, off, obj, probe, inten, tab)
 
 
 def body(object_slices, probe, position_count, offsets, intensities):
-    tab = jnp.asarray(tables())
-    count, off = position_count[0], offsets[0, 0]
-    inten = intensities[0, 0]
-    ext = halo(object_slices.reshape(4, 256, 256))
-    g, gp = compute(count, off, ext, probe, inten, tab)
-    ext, probe = step(False, g, gp, ext, probe)
-    g, gp = compute(count, off, ext, probe, inten, tab)
-    core, probe = step(True, g, gp, ext, probe)
-    return core.reshape(2, 2, 256, 256), probe
+    obj, probe = run(
+        position_count[0],
+        offsets[0, 0],
+        object_slices.reshape(4, 256, 256),
+        probe,
+        intensities[0, 0],
+        jnp.asarray(tables()),
+    )
+    return obj.reshape(2, 2, 256, 256), probe
 
 
 def solution(mesh):

time: 171 us -> 136 us (0.80)
  Pallas kernels: 164 us -> 130 us
    pallas_call x5 -> x1, Pallas kernels: 164 us -> 130 us  [run(): pl.pallas_call(program_kernel, out_shape=(jax.ShapeDtypeStruct((4, 256, 2...]
    unnamed x16 -> x4, local copies, waits for them, and re-layouts: 4.41 us -> 3.14 us
where the time goes in v2:
time: 136 us
  Pallas kernels  130 us (96%)
  local copies, waits for them, and re-layouts  4.49 us (3%)
    pallas_call x1, Pallas kernels, run(): pl.pallas_call(program_kernel, out_shape=(jax.ShapeDtypeStruct((4, 256, 2...  130 us
    unnamed x4, local copies, waits for them, and re-layouts  3.14 us

profile of v2, /device:TPU:1, one launch (start us, length us, event | category | flops | bytes accessed | tf_op | source)
XLA Modules:
  0.0 135.6 jit_solution(5177599492138992886)
XLA Ops:
  1.3 1.4 copy.8.off_ref
  2.6 129.8 %iterations.1 = (f32[4,256,256]{2,1,0:T(8,128)}, f32[2,256,256]{2,1,0:T(8,128)}) custom-call(s32[1]{0:T(128)} %bitcast.5.count_ref, s32[5,2]{1,0:T(8,128)} %copy.8.off_ref, f32[4,256,256]{2,1,0:T(8,128)} %bitcast.8, f32[2,256,256]{2,1,0:T(8,128)} %probe_in.1, f32[5,256,256]{2,1,0:T(8,128)} %bitcast.6, bf16[2,3,2,256,256]{4,3,2,1,0:T(8,128)(2,1)} %constant.2.clone.tab_hbm), custom_call_target="tpu_custom_call" | custom-call | tf_op jit(solution)/shard_map/iterations/pallas_call | solution.py:501
  132.5 0.0 copy-start
  132.5 2.3 %copy.12 = f32[2,2,256,256]{3,2,1,0:T(8,128)} copy(f32[2,2,256,256]{3,2,1,0:T(8,128)} %bitcast.7) | data formatting | bytes 2097152
  134.8 0.0 copy-done
  134.8 0.8 copy.13
Async XLA Ops:
  132.5 2.4 %copy-start = (f32[2,256,256]{2,1,0:T(8,128)S(1)}, f32[2,256,256]{2,1,0:T(8,128)}, u32[]{:S(2)}) copy-start(f32[2,256,256]{2,1,0:T(8,128)} %get-tuple-element.9) | copy-start | bytes 1572868

commit v3 on v2

v3 whole, which is shorter than its diff:
```python
import functools

import jax
import jax.numpy as jnp
import ml_dtypes
import numpy as np
from jax import lax
from jax.experimental import pallas as pl
from jax.experimental.pallas import tpu as pltpu
from jax.sharding import PartitionSpec as P

PROBE = 256
MAXPOS = 5
ITERS = 2
bf = jnp.bfloat16
f32 = jnp.float32

chirp_rate = 0.5
object_rate = 0.5
probe_rate = 2.0


def tables():
    n = PROBE
    k = np.arange(n)
    four = np.exp(-2j * np.pi * ((k[:, None] * k[None, :]) % n) / n) / np.sqrt(n)
    c = (((k + n // 2) % n) - n // 2).astype(np.float64)
    prop = (np.conj(four) * np.exp(-1j * chirp_rate * np.pi * c * c / n)[None, :]) @ four
    out = []
    for mat in (four, prop):
        real, imag = mat.real, mat.imag
        for part in (real, imag - real, real + imag):
            part = part.astype(np.float32)
            high = part.astype(ml_dtypes.bfloat16)
            out += [high, (part - high.astype(np.float32)).astype(ml_dtypes.bfloat16)]
    return np.stack(out).reshape(2, 3, 2, n, n)


def split(x):
    high = x.astype(bf)
    return high, (x - high.astype(f32)).astype(bf)


def dot(a, b):
    return jnp.dot(a, b, preferred_element_type=f32)


def left(tab, which, j, x):
    high, low = split(x)
    mat = jnp.concatenate([tab[which, j, 0], tab[which, j, 0], tab[which, j, 1]], axis=1)
    return dot(mat, jnp.concatenate([high, low, high], axis=0))


def right(tab, which, j, x):
    high, low = split(x)
    mat = jnp.concatenate([tab[which, j, 0], tab[which, j, 0], tab[which, j, 1]], axis=0)
    return dot(jnp.concatenate([high, low, high], axis=1), mat)


def sandwich(tab, which, real, imag, mid):
    shared = left(tab, which, 0, real + imag)
    mid[1] = shared + left(tab, which, 1, real)
    mid[0] = shared - left(tab, which, 2, imag)
    real, imag = mid[0], mid[1]
    shared = right(tab, which, 0, real + imag)
    return shared - right(tab, which, 2, imag), shared + right(tab, which, 1, real)


NTY, NTX = 8, 16
MESH = pl.DeviceIdType.MESH
DIRS = [(dy, dx) for dy in (-1, 0, 1) for dx in (-1, 0, 1) if (dy, dx) != (0, 0)]
V = pl.BlockSpec(memory_space=pltpu.VMEM)


def half_lanes(shape):
    return lax.broadcasted_iota(jnp.int32, shape, len(shape) - 1) < 64


def pack(x, side):
    rows = x.shape[1] // 2
    first, second = x[:, :rows], x[:, rows:]
    low = half_lanes(first.shape)
    if side > 0:
        return jnp.where(low, pltpu.roll(first, 64, 2), second)
    return jnp.where(low, first, pltpu.roll(second, 64, 2))


def unpack(buf, side):
    turned = pltpu.roll(buf, 64, 2)
    pair = [turned, buf] if side > 0 else [buf, turned]
    return jnp.concatenate(pair, axis=1)


def keep_side(x, side):
    low = half_lanes(x.shape)
    return jnp.where(low, 0.0, x) if side > 0 else jnp.where(low, x, 0.0)


class Place:
    def __init__(self):
        self.ty, self.tx = lax.axis_index("ty"), lax.axis_index("tx")
        self.x_lo, self.y = self.ty // 4, lax.rem(self.ty, 4)
        self.z, self.core = self.tx // 4, lax.rem(self.tx, 2)
        self.x_hi = lax.rem(self.tx // 2, 2)
        self.x = self.x_hi * 2 + self.x_lo

    def neighbour(self, dy, dx):
        return (lax.rem(self.ty + dy + NTY, NTY), lax.rem(self.tx + dx + NTX, NTX))

    def sibling(self):
        return (self.ty, self.tx + 1 - 2 * self.core)

    def turn(self, axis, k):
        x, y, z = self.x, self.y, self.z
        if axis == "x":
            x = lax.rem(x + k, 4)
        elif axis == "y":
            y = lax.rem(y + k, 4)
        else:
            z = lax.rem(z + k, 4)
        spot = {"x": x, "y": y, "z": z}[axis]
        return spot, (lax.rem(x, 2) * 4 + y, z * 4 + (x // 2) * 2 + self.core)


def remote(src, dst, send, recv, device):
    return pltpu.make_async_remote_copy(
        src_ref=src, dst_ref=dst, send_sem=send, recv_sem=recv, device_id=device, device_id_type=MESH
    )


class Edges:
    def __init__(self, place, rows, cols, corners, sems):
        self.place, self.rows, self.cols, self.corners = place, rows, cols, corners
        self.send, self.recv = sems

    def slot(self, bufs, dy, dx):
        if dx == 0:
            return bufs[0].at[(dy + 1) // 2]
        if dy == 0:
            return bufs[1].at[(dx + 1) // 2]
        return bufs[2].at[(dy + 1) + (dx + 1) // 2]

    def out(self, dy, dx):
        return self.slot((self.rows[0], self.cols[0], self.corners[0]), dy, dx)

    def inc(self, dy, dx):
        return self.slot((self.rows[1], self.cols[1], self.corners[1]), dy, dx)

    def copy(self, dy, dx):
        i = DIRS.index((dy, dx))
        return remote(self.out(dy, dx), self.inc(dy, dx), self.send.at[i], self.recv.at[i], self.place.neighbour(dy, dx))


ORDER = [(0, 1), (0, -1), (1, 0), (-1, 0), (1, 1), (1, -1), (-1, 1), (-1, -1)]


def pack_halo(e, core):
    for dy, dx in ORDER:
        r0, r1 = {-1: (0, 64), 0: (0, 256), 1: (192, 256)}[dy]
        if dx == 0:
            for t in range(2):
                e.out(dy, dx)[:, t] = core(t, r0, r1)
        else:
            e.out(dy, dx)[...] = pack(core((dx + 1) // 2, r0, r1), dx)


def unpack_halo(e, ext):
    for dy, dx in ORDER:
        e.copy(dy, dx).wait_recv()
    for dy in (-1, 1):
        r0 = 320 if dy < 0 else 0
        for t in range(2):
            ext[:, t, r0 : r0 + 64] = e.inc(dy, 0)[:, t]
    for dy in (-1, 0, 1):
        r0, r1 = {-1: (320, 384), 0: (64, 320), 1: (0, 64)}[dy]
        left, right = unpack(e.inc(dy, -1)[...], -1), unpack(e.inc(dy, 1)[...], 1)
        ext[:, 2, r0:r1] = jnp.where(half_lanes(left.shape), left, right)


def pack_fold(e, g):
    for dy, dx in ORDER:
        r0, r1 = {-1: (0, 64), 0: (64, 320), 1: (320, 384)}[dy]
        if dx == 0:
            for t in range(2):
                e.out(dy, dx)[:, t] = g[:, t, r0:r1]
        else:
            e.out(dy, dx)[...] = pack(g[:, 2, r0:r1], -dx)


def fold(e, g, total):
    for dy, dx in ORDER:
        e.copy(dy, dx).wait_recv()
    for t in range(2):
        total[:, t] = g[:, t, 64:320]
    for dy, dx in ORDER:
        r0, r1 = {-1: (192, 256), 0: (0, 256), 1: (0, 64)}[dy]
        if dx == 0:
            for t in range(2):
                total[:, t, r0:r1] += e.inc(dy, dx)[:, t]
        else:
            t = (1 - dx) // 2
            total[:, t, r0:r1] += keep_side(unpack(e.inc(dy, dx)[...], -dx), -dx)


def start_all(e):
    for dy, dx in ORDER:
        e.copy(dy, dx).start()


def wait_sent(e):
    for dy, dx in ORDER:
        e.copy(dy, dx).wait_send()


class Summer:
    def __init__(self, place, gp, bufs, sems):
        self.p, self.gp = place, gp
        self.pair, self.made, self.zin, self.ysum, self.yin, self.cross, self.whole = bufs
        self.send, self.recv = sems
        self.zs = [place.turn("z", k) for k in range(4)]
        self.ys = [place.turn("y", k) for k in range(4)]
        self.xs = [place.turn("x", k) for k in range(4)]

    def copy(self, phase, k, src, dst, device):
        return remote(src, dst, self.send.at[phase, k], self.recv.at[phase, k], device)

    def pair_copy(self, k):
        z = self.zs[k][0]
        return self.copy(0, k, self.gp.at[1 - self.p.core, z], self.pair.at[z], self.p.sibling())

    def z_copy(self, k):
        z, device = self.zs[k]
        return self.copy(1, k, self.made.at[k], self.zin.at[k], device)

    def y_copy(self, k):
        y, device = self.ys[k]
        return self.copy(2, k, self.ysum.at[y], self.yin.at[k], device)

    def x_copy(self, k):
        own = self.cross.at[self.p.x]
        return self.copy(3, k, own, own, self.xs[k][1])

    def y_back(self, k):
        own = self.whole.at[self.p.core, self.p.z, self.p.y]
        return self.copy(4, k, own, own, self.ys[k][1])

    def z_back(self, k):
        own = self.whole.at[self.p.core, self.p.z]
        return self.copy(5, k, own, own, self.zs[k][1])

    def forward_copy(self, k):
        own = self.whole.at[self.p.core, self.zs[(4 - k) % 4][0]]
        return self.copy(6, k, own, own, self.p.sibling())

    def begin(self):
        for k in (1, 2, 3, 0):
            self.pair_copy(k).start()

    def over_z(self):
        for k in (1, 2, 3, 0):
            z = self.zs[k][0]
            self.pair_copy(k).wait_recv()
            self.made[k] = self.gp[self.p.core, z] + self.pair[z]
            if k:
                self.z_copy(k).start()

    def over_y(self):
        for k in (1, 2, 3):
            self.z_copy(k).wait_recv()
        self.ysum[...] = (self.made[0] + self.zin[1]) + (self.zin[2] + self.zin[3])
        for k in (1, 2, 3):
            self.y_copy(k).start()

    def over_x(self):
        for k in (1, 2, 3):
            self.y_copy(k).wait_recv()
        self.cross[self.p.x] = (self.ysum[self.p.y] + self.yin[1]) + (self.yin[2] + self.yin[3])
        for k in (1, 2, 3):
            self.x_copy(k).start()

    def gather_y(self):
        for k in (1, 2, 3):
            self.x_copy(k).wait_recv()
        own = (self.cross[0] + self.cross[1]) + (self.cross[2] + self.cross[3])
        self.whole[self.p.core, self.p.z, self.p.y] = own
        for k in (1, 2, 3):
            self.y_back(k).start()

    def gather_z(self):
        for k in (1, 2, 3):
            self.y_back(k).wait_recv()
        for k in (1, 2, 3):
            self.z_back(k).start()
        self.forward_copy(0).start()

    def gather_pair(self):
        for k in (1, 2, 3):
            self.z_back(k).wait_recv()
            self.forward_copy(k).start()

    def finish(self):
        for k in range(4):
            self.forward_copy(k).wait_recv()

    def sent(self):
        for k in range(4):
            self.pair_copy(k).wait_send()
            self.forward_copy(k).wait_send()
        for k in (1, 2, 3):
            for copy in (self.z_copy, self.y_copy, self.x_copy, self.y_back, self.z_back):
                copy(k).wait_send()


def greet(p):
    barrier = pltpu.get_barrier_semaphore()
    devices = [p.neighbour(dy, dx) for dy, dx in DIRS] + [p.sibling()]
    devices += [p.turn(axis, k)[1] for axis in "xyz" for k in (1, 2, 3)]
    for device in devices:
        pl.semaphore_signal(barrier, inc=1, device_id=device, device_id_type=MESH)
    return lambda: pl.semaphore_wait(barrier, len(devices))


EXCHANGES = 8
SUMS = ITERS


def exchange(p, refs, i):
    rows, cols, corners, sems = [ref.at[i] for ref in refs]
    pair = lambda ref: (ref.at[0], ref.at[1])
    return Edges(p, pair(rows), pair(cols), pair(corners), pair(sems))


def shifts(off_ref, s):
    top, left_col = off_ref[0, s], off_ref[1, s]
    inner = left_col >= 64
    first = jnp.where(inner, 0, 2)
    second = jnp.where(inner, 1, 0)
    third = jnp.where(inner, 2, 1)
    return top, jnp.where(inner, left_col - 64, left_col + 64), (first, second, third)


def take_window(off_ref, s, ext, win):
    top, shift, tiles = shifts(off_ref, s)
    keep = lax.broadcasted_iota(jnp.int32, (256, 128), 1) < 128 - shift
    for p in range(2):
        a, b, c = [pltpu.roll(ext[p, t, pl.ds(top, 256), :], 128 - shift, 1) for t in tiles]
        win[s, p, :, 0:128] = jnp.where(keep, a, b)
        win[s, p, :, 128:256] = jnp.where(keep, b, c)


def add_window(off_ref, count_ref, s, pair, slide, acc):
    top, shift, (first, second, third) = shifts(off_ref, s)
    lane = lax.broadcasted_iota(jnp.int32, (256, 128), 1)
    before = lane < shift
    active = lane * 0 + s < count_ref[0, 0]
    for p in range(2):
        a, b = [
            pltpu.roll(jnp.where(active, pair[p][:, t * 128 : t * 128 + 128], 0.0), shift, 1) for t in range(2)
        ]
        slide[p, 0, 128:384] = jnp.where(before, 0.0, a)
        slide[p, 1, 128:384] = jnp.where(before, a, b)
        slide[p, 2, 128:384] = jnp.where(before, b, 0.0)
    inner = first == 0
    source = (jnp.where(inner, 0, 1), jnp.where(inner, 1, 2), jnp.where(inner, 2, 0))
    for p in range(2):
        for t in range(3):
            acc[p, t] += slide[p, source[t], pl.ds(128 - top, 384), :]


def each_slot(fn):
    for s in range(MAXPOS):
        fn(s)


def program_kernel(
    count_ref, off_ref, obj, probe_in, inten_hbm, tab_hbm, obj_out, probe_out,
    tab, inten, ext1, ext2, acc1, acc2, gp, slides, win1, win2, moved, back, mids, total, probe,
    rows, cols, corners, edge_sems, pair, made, zin, ysum, yin, cross, whole, sum_sems, local_sems,
):
    p = Place()
    ready = greet(p)
    edges = (rows, cols, corners, edge_sems)
    tab_copy = pltpu.make_async_copy(tab_hbm, tab, local_sems.at[0])
    inten_copy = pltpu.make_async_copy(inten_hbm, inten, local_sems.at[1])
    tab_copy.start()
    inten_copy.start()
    halo1, halo2 = exchange(p, edges, 0), exchange(p, edges, 1)
    pack_halo(halo1, lambda t, r0, r1: obj[0:2, r0:r1, t * 128 : t * 128 + 128])
    ready()
    start_all(halo1)
    pack_halo(halo2, lambda t, r0, r1: obj[2:4, r0:r1, t * 128 : t * 128 + 128])
    start_all(halo2)
    for t in range(2):
        ext1[:, t, 64:320] = obj[0:2, :, t * 128 : t * 128 + 128]
        ext2[:, t, 64:320] = obj[2:4, :, t * 128 : t * 128 + 128]
    slides[...] = jnp.zeros_like(slides)
    obj_out[...] = jnp.zeros_like(obj_out)
    probe_out[...] = jnp.zeros_like(probe_out)
    probe[...] = probe_in[...]
    tab_copy.wait()
    inten_copy.wait()
    unpack_halo(halo1, ext1)

    def iteration(it, carry):
        acc1[...] = jnp.zeros_like(acc1)
        acc2[...] = jnp.zeros_like(acc2)
        gp[...] = jnp.zeros_like(gp)

        def forward(s):
            take_window(off_ref, s, ext1, win1)
            pr, pi, wr, wi = probe[0], probe[1], win1[s, 0], win1[s, 1]
            moved[s, 0], moved[s, 1] = sandwich(tab, 1, pr * wr - pi * wi, pr * wi + pi * wr, mids.at[s])

        def detector(s):
            take_window(off_ref, s, ext2, win2)
            er = moved[s, 0] * win2[s, 0] - moved[s, 1] * win2[s, 1]
            ei = moved[s, 0] * win2[s, 1] + moved[s, 1] * win2[s, 0]
            fr, fi = sandwich(tab, 0, er, ei, mids.at[s])
            misfit = fr * fr + fi * fi - inten[s]
            cr, ci = sandwich(tab, 0, misfit * fr, -(misfit * fi), mids.at[s])
            back[s, 0] = win2[s, 0] * cr - win2[s, 1] * ci
            back[s, 1] = win2[s, 0] * ci + win2[s, 1] * cr
            g2 = (moved[s, 0] * cr - moved[s, 1] * ci, -(moved[s, 0] * ci + moved[s, 1] * cr))
            add_window(off_ref, count_ref, s, g2, slides.at[s % 2], acc2)

        def adjoint(s):
            wr, wi = sandwich(tab, 1, back[s, 0], back[s, 1], mids.at[s])
            g1 = (probe[0] * wr - probe[1] * wi, -(probe[0] * wi + probe[1] * wr))
            add_window(off_ref, count_ref, s, g1, slides.at[s % 2], acc1)
            active = lax.broadcasted_iota(jnp.int32, (256, 128), 1) * 0 + s < count_ref[0, 0]
            parts = (win1[s, 0] * wr - win1[s, 1] * wi, -(win1[s, 0] * wi + win1[s, 1] * wr))
            for h in range(2):
                for t in range(2):
                    part = jnp.where(active, parts[h][:, t * 128 : t * 128 + 128], 0.0)
                    gp[h, 2 * t : 2 * t + 2] += part.reshape(2, 4, 32, 128)

        each_slot(forward)
        unpack_halo(exchange(p, edges, 4 * it + 1), ext2)
        each_slot(detector)
        fold2, fold1 = exchange(p, edges, 4 * it + 2), exchange(p, edges, 4 * it + 3)
        pack_fold(fold2, acc2)
        start_all(fold2)
        each_slot(adjoint)

        bufs = [ref.at[it] for ref in (pair, made, zin, ysum, yin, cross, whole)]
        s = Summer(p, gp, bufs, (sum_sems.at[it, 0], sum_sems.at[it, 1]))
        s.begin()
        pack_fold(fold1, acc1)
        start_all(fold1)
        s.over_z()
        rate = step_size(probe)

        def update(e, acc, ext, first):
            fold(e, acc, total)
            for t in range(2):
                change = rate * total[:, t]
                ext[:, t, 64:320] -= change
                obj_out[first : first + 2, :, t * 128 : t * 128 + 128] += change

        update(fold2, acc2, ext2, 2)
        s.over_y()
        s.over_x()
        update(fold1, acc1, ext1, 0)

        @pl.when(it == 0)
        def _():
            halo = exchange(p, edges, 4)
            pack_halo(halo, lambda t, r0, r1: ext1[:, t, 64 + r0 : 64 + r1])
            start_all(halo)

        s.gather_y()

        @pl.when(it == 0)
        def _():
            halo = exchange(p, edges, 5)
            pack_halo(halo, lambda t, r0, r1: ext2[:, t, 64 + r0 : 64 + r1])
            start_all(halo)

        s.gather_z()
        s.gather_pair()

        @pl.when(it == 0)
        def _():
            unpack_halo(exchange(p, edges, 4), ext1)

        s.finish()
        for h in range(2):
            for t in range(2):
                lanes = slice(t * 128, t * 128 + 128)
                change = (probe_rate / (NTY * NTX)) * s.whole[h, 2 * t : 2 * t + 2].reshape(256, 128)
                probe[h, :, lanes] -= change
                probe_out[h, :, lanes] += change
        s.sent()
        return carry

    lax.fori_loop(0, ITERS, iteration, 0)
    for i in range(EXCHANGES):
        wait_sent(exchange(p, edges, i))


def step_size(probe):
    power = probe[0] * probe[0] + probe[1] * probe[1]
    peak = jnp.max(power, axis=(0, 1), keepdims=True) + 1e-06
    return object_rate / peak


def run(count, off, obj, probe, inten, tab):
    smem = pl.BlockSpec(memory_space=pltpu.SMEM)
    anywhere = pl.BlockSpec(memory_space=pl.ANY)
    vm = pltpu.VMEM
    slots = vm((MAXPOS, 2, 256, 256), f32)
    return pl.pallas_call(
        program_kernel,
        out_shape=(jax.ShapeDtypeStruct((4, 256, 256), f32), jax.ShapeDtypeStruct((2, 256, 256), f32)),
        in_specs=[smem, smem, V, V, anywhere, anywhere],
        out_specs=(V, V),
        scratch_shapes=[
            vm((2, 3, 2, 256, 256), bf),
            vm((MAXPOS, 256, 256), f32),
            vm((2, 3, 384, 128), f32),
            vm((2, 3, 384, 128), f32),
            vm((2, 3, 384, 128), f32),
            vm((2, 3, 384, 128), f32),
            vm((2, 4, 4, 32, 128), f32),
            vm((2, 2, 3, 512, 128), f32),
            slots,
            slots,
            slots,
            slots,
            slots,
            vm((2, 2, 256, 128), f32),
            vm((2, 256, 256), f32),
            vm((EXCHANGES, 2, 2, 2, 2, 64, 128), f32),
            vm((EXCHANGES, 2, 2, 2, 128, 128), f32),
            vm((EXCHANGES, 2, 4, 2, 32, 128), f32),
            pltpu.SemaphoreType.DMA((EXCHANGES, 2, 8)),
            vm((SUMS, 4, 4, 32, 128), f32),
            vm((SUMS, 4, 4, 32, 128), f32),
            vm((SUMS, 4, 4, 32, 128), f32),
            vm((SUMS, 4, 32, 128), f32),
            vm((SUMS, 4, 32, 128), f32),
            vm((SUMS, 4, 32, 128), f32),
            vm((SUMS, 2, 4, 4, 32, 128), f32),
            pltpu.SemaphoreType.DMA((SUMS, 2, 7, 4)),
            pltpu.SemaphoreType.DMA((2,)),
        ],
        compiler_params=pltpu.CompilerParams(collective_id=0, has_side_effects=True, vmem_limit_bytes=50 << 20),
        name="iterations",
    )(count, off, obj, probe, inten, tab)


def body(object_slices, probe, position_count, offsets, intensities):
    obj_change, probe_change = run(
        position_count,
        offsets[0, 0].T,
        object_slices.reshape(4, 256, 256),
        probe,
        intensities[0, 0],
        jnp.asarray(tables()),
    )
    return object_slices - obj_change.reshape(2, 2, 256, 256), probe - probe_change


def solution(mesh):
    placed = (
        P(None, None, "ty", "tx"),
        P(),
        P("ty", "tx"),
        P("ty", "tx", None, None),
        P("ty", "tx", None, None, None),
    )
    return jax.shard_map(
        body,
        mesh=mesh,
        in_specs=placed,
        out_specs=(P(None, None, "ty", "tx"), P()),
        check_vma=False,
    )
```

time: 136 us -> 126 us (0.926)
  Pallas kernels: 130 us -> 119 us
  other arithmetic: 0 us -> 1.97 us
  local copies, waits for them, and re-layouts: 4.49 us -> 2.94 us
    pallas_call x1, Pallas kernels: 130 us -> 119 us  [run(): pl.pallas_call(program_kernel, out_shape=(jax.ShapeDtypeStruct((4, 256, 2...]
    sub x0 -> x2, other arithmetic: none -> 1.97 us  [the longest x1 1.11 us: body(): object_slices - obj_change.reshape(2, 2, 256, 256)]
    unnamed x4 -> x6, local copies, waits for them, and re-layouts: 3.14 us -> 2.94 us
where the time goes in v3:
time: 126 us; the launch traced here: 125 us
  Pallas kernels  119 us (94%)
  local copies, waits for them, and re-layouts  2.94 us (2%)
  other arithmetic  1.97 us (2%)
  between operations  1.3 us (1%)
    pallas_call x1, Pallas kernels, run(): pl.pallas_call(program_kernel, out_shape=(jax.ShapeDtypeStruct((4, 256, 2...  119 us
    unnamed x6, local copies, waits for them, and re-layouts  2.94 us

profile of v3, /device:TPU:1, one launch (start us, length us, event | category | flops | bytes accessed | tf_op | source)
XLA Modules:
  0.0 125.5 jit_solution(16114153168360149638)
XLA Ops:
  1.3 0.0 copy-start
  1.3 1.2 copy-done
  2.5 0.0 copy-start.1
  2.5 1.0 copy-done.1
  3.5 0.0 copy-start.2
  3.5 0.7 copy-done.2
  4.2 119.3 %iterations.1 = (f32[4,256,256]{2,1,0:T(8,128)S(1)}, f32[2,256,256]{2,1,0:T(8,128)S(1)}) custom-call(s32[1,1]{1,0:T(1,128)S(6)} %copy.8.count_ref, s32[2,5]{1,0:T(2,128)S(1)} %bitcast.8, f32[4,256,256]{2,1,0:T(8,128)S(1)} %bitcast.6, f32[2,256,256]{2,1,0:T(8,128)S(1)} %copy-done.1, f32[5,256,256]{2,1,0:T(8,128)} %bitcast.9, ...), custom_call_target="tpu_custom_call" | custom-call | tf_op jit(solution)/shard_map/iterations/pallas_call | solution.py:512
  123.5 1.1 sub.6
  124.6 0.9 sub.7
Async XLA Ops:
  1.3 1.2 copy-start
  2.5 1.0 copy-start.1
  3.5 0.7 copy-start.2

commit v4 on v3

v4 whole, which is shorter than its diff:
```python
import functools

import jax
import jax.numpy as jnp
import ml_dtypes
import numpy as np
from jax import lax
from jax.experimental import pallas as pl
from jax.experimental.pallas import tpu as pltpu
from jax.sharding import PartitionSpec as P

PROBE = 256
MAXPOS = 5
ITERS = 2
bf = jnp.bfloat16
f32 = jnp.float32

chirp_rate = 0.5
object_rate = 0.5
probe_rate = 2.0


def tables():
    n = PROBE
    k = np.arange(n)
    angle = 2 * np.pi * ((k[:, None] * k[None, :]) % n) / n
    four = np.exp(-1j * angle) / np.sqrt(n)
    c = (((k + n // 2) % n) - n // 2).astype(np.float64)
    prop = (np.conj(four) * np.exp(-1j * chirp_rate * np.pi * c * c / n)[None, :]) @ four
    order = np.concatenate([k[: n // 2], [n // 2], k[: n // 2 : -1]])
    hartley = ((np.cos(angle) + np.sin(angle)) / np.sqrt(2 * n))[order]
    swap = np.eye(n)[order]
    out = []
    for part in (prop.real, prop.imag - prop.real, prop.real + prop.imag, hartley, hartley.T):
        part = part.astype(np.float32)
        high = part.astype(ml_dtypes.bfloat16)
        out.append(np.stack([high, (part - high.astype(np.float32)).astype(ml_dtypes.bfloat16)]))
    out.append(np.stack([swap, swap.T]).astype(ml_dtypes.bfloat16))
    return np.stack(out)


def split(x):
    high = x.astype(bf)
    return high, (x - high.astype(f32)).astype(bf)


def dot(a, b):
    return jnp.dot(a, b, preferred_element_type=f32)


def left(tab, j, x):
    high, low = split(x)
    mat = jnp.concatenate([tab[j, 0], tab[j, 0], tab[j, 1]], axis=1)
    return dot(mat, jnp.concatenate([high, low, high], axis=0))


def right(tab, j, x):
    high, low = split(x)
    mat = jnp.concatenate([tab[j, 0], tab[j, 0], tab[j, 1]], axis=0)
    return dot(jnp.concatenate([high, low, high], axis=1), mat)


def propagate(tab, real, imag, mid):
    shared = left(tab, 0, real + imag)
    mid[1] = shared + left(tab, 1, real)
    mid[0] = shared - left(tab, 2, imag)
    real, imag = mid[0], mid[1]
    shared = right(tab, 0, real + imag)
    return shared - right(tab, 2, imag), shared + right(tab, 1, real)


def hartley(tab, j, real, imag, mid):
    mid[0], mid[1] = left(tab, j, real), left(tab, j, imag)
    return right(tab, 7 - j, mid[0]), right(tab, 7 - j, mid[1])


def mirror_rows(z):
    top, bottom = z[:128], z[128:]
    first = lax.broadcasted_iota(jnp.int32, (8, 256), 0) == 0
    new_top = jnp.where(first, top[:8], bottom[:8])
    new_bottom = jnp.where(first, bottom[:8], top[:8])
    return jnp.concatenate([new_top, bottom[8:], new_bottom, top[8:]], axis=0)


def mirror_columns(z):
    near, far = z[:, :128], z[:, 128:]
    first = lax.broadcasted_iota(jnp.int32, (256, 128), 1) == 0
    return jnp.concatenate([jnp.where(first, near, far), jnp.where(first, far, near)], axis=1)


def combine(real, imag):
    pairs = []
    for z in (real, imag):
        across = mirror_columns(z)
        pairs.append((mirror_rows(z) + across, z - mirror_rows(across)))
    (even_r, odd_r), (even_i, odd_i) = pairs
    return even_r + odd_i, even_i - odd_r


def into_paired_order(tab, x):
    for side in range(2):
        high, low = split(x)
        rest = (x - high.astype(f32) - low.astype(f32)).astype(bf)
        if side == 0:
            x = dot(tab[5, 0], high) + dot(tab[5, 0], low) + dot(tab[5, 0], rest)
        else:
            x = dot(high, tab[5, 1]) + dot(low, tab[5, 1]) + dot(rest, tab[5, 1])
    return x


NTY, NTX = 8, 16
MESH = pl.DeviceIdType.MESH
DIRS = [(dy, dx) for dy in (-1, 0, 1) for dx in (-1, 0, 1) if (dy, dx) != (0, 0)]
V = pl.BlockSpec(memory_space=pltpu.VMEM)


def half_lanes(shape):
    return lax.broadcasted_iota(jnp.int32, shape, len(shape) - 1) < 64


def pack(x, side):
    rows = x.shape[1] // 2
    first, second = x[:, :rows], x[:, rows:]
    low = half_lanes(first.shape)
    if side > 0:
        return jnp.where(low, pltpu.roll(first, 64, 2), second)
    return jnp.where(low, first, pltpu.roll(second, 64, 2))


def unpack(buf, side):
    turned = pltpu.roll(buf, 64, 2)
    pair = [turned, buf] if side > 0 else [buf, turned]
    return jnp.concatenate(pair, axis=1)


def keep_side(x, side):
    low = half_lanes(x.shape)
    return jnp.where(low, 0.0, x) if side > 0 else jnp.where(low, x, 0.0)


class Place:
    def __init__(self):
        self.ty, self.tx = lax.axis_index("ty"), lax.axis_index("tx")
        self.x_lo, self.y = self.ty // 4, lax.rem(self.ty, 4)
        self.z, self.core = self.tx // 4, lax.rem(self.tx, 2)
        self.x_hi = lax.rem(self.tx // 2, 2)
        self.x = self.x_hi * 2 + self.x_lo

    def neighbour(self, dy, dx):
        return (lax.rem(self.ty + dy + NTY, NTY), lax.rem(self.tx + dx + NTX, NTX))

    def sibling(self):
        return (self.ty, self.tx + 1 - 2 * self.core)

    def turn(self, axis, k):
        x, y, z = self.x, self.y, self.z
        if axis == "x":
            x = lax.rem(x + k, 4)
        elif axis == "y":
            y = lax.rem(y + k, 4)
        else:
            z = lax.rem(z + k, 4)
        spot = {"x": x, "y": y, "z": z}[axis]
        return spot, (lax.rem(x, 2) * 4 + y, z * 4 + (x // 2) * 2 + self.core)


def remote(src, dst, send, recv, device):
    return pltpu.make_async_remote_copy(
        src_ref=src, dst_ref=dst, send_sem=send, recv_sem=recv, device_id=device, device_id_type=MESH
    )


class Edges:
    def __init__(self, place, rows, cols, corners, sems):
        self.place, self.rows, self.cols, self.corners = place, rows, cols, corners
        self.send, self.recv = sems

    def slot(self, bufs, dy, dx):
        if dx == 0:
            return bufs[0].at[(dy + 1) // 2]
        if dy == 0:
            return bufs[1].at[(dx + 1) // 2]
        return bufs[2].at[(dy + 1) + (dx + 1) // 2]

    def out(self, dy, dx):
        return self.slot((self.rows[0], self.cols[0], self.corners[0]), dy, dx)

    def inc(self, dy, dx):
        return self.slot((self.rows[1], self.cols[1], self.corners[1]), dy, dx)

    def copy(self, dy, dx):
        i = DIRS.index((dy, dx))
        return remote(self.out(dy, dx), self.inc(dy, dx), self.send.at[i], self.recv.at[i], self.place.neighbour(dy, dx))


ORDER = [(1, 1), (1, -1), (-1, 1), (-1, -1), (0, 1), (0, -1), (1, 0), (-1, 0)]


def send_halo(e, core, ready=None):
    for dy, dx in ORDER:
        r0, r1 = {-1: (0, 64), 0: (0, 256), 1: (192, 256)}[dy]
        if dx == 0:
            for t in range(2):
                e.out(dy, dx)[:, t] = core(t, r0, r1)
        else:
            e.out(dy, dx)[...] = pack(core((dx + 1) // 2, r0, r1), dx)
        if ready is None:
            e.copy(dy, dx).start()
    if ready is not None:
        ready()
        for dy, dx in ORDER:
            e.copy(dy, dx).start()


def unpack_halo(e, ext):
    for dy in (-1, 1):
        e.copy(dy, 0).wait_recv()
        r0 = 320 if dy < 0 else 0
        for t in range(2):
            ext[:, t, r0 : r0 + 64] = e.inc(dy, 0)[:, t]
    for dy in (0, -1, 1):
        e.copy(dy, -1).wait_recv()
        e.copy(dy, 1).wait_recv()
        r0, r1 = {-1: (320, 384), 0: (64, 320), 1: (0, 64)}[dy]
        left, right = unpack(e.inc(dy, -1)[...], -1), unpack(e.inc(dy, 1)[...], 1)
        ext[:, 2, r0:r1] = jnp.where(half_lanes(left.shape), left, right)


def send_fold(e, g):
    for dy, dx in ORDER:
        r0, r1 = {-1: (0, 64), 0: (64, 320), 1: (320, 384)}[dy]
        if dx == 0:
            for t in range(2):
                e.out(dy, dx)[:, t] = g[:, t, r0:r1]
        else:
            e.out(dy, dx)[...] = pack(g[:, 2, r0:r1], -dx)
        e.copy(dy, dx).start()


def step_down(ext, t, r0, r1, change):
    ext[:, t, 64 + r0 : 64 + r1] -= change


def descend_own(g, ext, rate):
    for t in range(2):
        step_down(ext, t, 0, 256, rate * g[:, t, 64:320])


def descend(e, ext, rate):
    for dy, dx in ORDER[4:] + ORDER[:4]:
        e.copy(dy, dx).wait_recv()
        r0, r1 = {-1: (192, 256), 0: (0, 256), 1: (0, 64)}[dy]
        if dx == 0:
            for t in range(2):
                step_down(ext, t, r0, r1, rate * e.inc(dy, dx)[:, t])
        else:
            values = keep_side(unpack(e.inc(dy, dx)[...], -dx), -dx)
            step_down(ext, (1 - dx) // 2, r0, r1, rate * values)


def wait_sent(e):
    for dy, dx in ORDER:
        e.copy(dy, dx).wait_send()


class Summer:
    def __init__(self, place, gp, bufs, sems):
        self.p, self.gp = place, gp
        self.pair, self.made, self.parts, self.cross, self.whole = bufs
        self.send, self.recv = sems
        self.zs = [place.turn("z", k)[0] for k in range(4)]
        self.ys = [place.turn("y", k)[0] for k in range(4)]
        self.xs = [place.turn("x", k)[1] for k in range(4)]

    def copy(self, i, src, dst, device):
        return remote(src, dst, self.send.at[i], self.recv.at[i], device)

    def device(self, k, j):
        return (self.p.x_lo * 4 + self.ys[j], self.zs[k] * 4 + self.p.x_hi * 2 + self.p.core)

    def pair_copy(self, k):
        z = self.zs[k]
        return self.copy(k, self.gp.at[1 - self.p.core, z], self.pair.at[z], self.p.sibling())

    def plane_copy(self, k, j):
        return self.copy(8 + 4 * k + j, self.made.at[k, self.ys[j]], self.parts.at[k, j], self.device(k, j))

    def x_copy(self, k):
        own = self.cross.at[self.p.x]
        return self.copy(40 + k, own, own, self.xs[k])

    def back_copy(self, k, j):
        own = self.whole.at[self.p.core, self.p.z, self.p.y]
        return self.copy(24 + 4 * k + j, own, own, self.device(k, j))

    def forward_copy(self, k):
        own = self.whole.at[self.p.core, self.zs[(4 - k) % 4]]
        return self.copy(4 + k, own, own, self.p.sibling())

    def begin(self):
        for k in (2, 1, 3, 0):
            self.pair_copy(k).start()

    def over_plane(self):
        for k in (2, 1, 3, 0):
            z = self.zs[k]
            self.pair_copy(k).wait_recv()
            self.made[k] = self.gp[self.p.core, z] + self.pair[z]
            for j in (2, 1, 3, 0):
                if k or j:
                    self.plane_copy(k, j).start()

    def over_x(self):
        total = self.made[0, self.p.y]
        for k in (0, 1, 3, 2):
            for j in (0, 1, 3, 2):
                if k or j:
                    self.plane_copy(k, j).wait_recv()
                    total = total + self.parts[k, j]
        self.cross[self.p.x] = total
        for k in (2, 1, 3):
            self.x_copy(k).start()

    def spread(self):
        for k in (1, 3, 2):
            self.x_copy(k).wait_recv()
        own = (self.cross[0] + self.cross[1]) + (self.cross[2] + self.cross[3])
        self.whole[self.p.core, self.p.z, self.p.y] = own
        for k in (2, 1, 3, 0):
            for j in (2, 1, 3, 0):
                if k or j:
                    self.back_copy(k, j).start()

    def gather_pair(self):
        for k in (0, 1, 3, 2):
            for j in range(4):
                if k or j:
                    self.back_copy(k, j).wait_recv()
            self.forward_copy(k).start()

    def finish(self):
        for k in range(4):
            self.forward_copy(k).wait_recv()
            self.pair_copy(k).wait_send()

    def sent(self):
        for k in range(4):
            self.forward_copy(k).wait_send()
            for j in range(4):
                if k or j:
                    self.plane_copy(k, j).wait_send()
                    self.back_copy(k, j).wait_send()
        for k in (1, 2, 3):
            self.x_copy(k).wait_send()


def greet(p):
    barrier = pltpu.get_barrier_semaphore()
    devices = [p.neighbour(dy, dx) for dy, dx in DIRS] + [p.sibling()]
    devices += [p.turn("x", k)[1] for k in (1, 2, 3)]
    for k in range(4):
        z = p.turn("z", k)[0]
        for j in range(4):
            if k or j:
                devices.append((p.x_lo * 4 + p.turn("y", j)[0], z * 4 + p.x_hi * 2 + p.core))
    for device in devices:
        pl.semaphore_signal(barrier, inc=1, device_id=device, device_id_type=MESH)
    return lambda: pl.semaphore_wait(barrier, len(devices))


EXCHANGES = 8
SUMS = ITERS


def exchange(p, refs, i):
    rows, cols, corners, sems = [ref.at[i] for ref in refs]
    pair = lambda ref: (ref.at[0], ref.at[1])
    return Edges(p, pair(rows), pair(cols), pair(corners), pair(sems))


def shifts(off_ref, s):
    top, left_col = off_ref[0, s], off_ref[1, s]
    inner = left_col >= 64
    first = jnp.where(inner, 0, 2)
    second = jnp.where(inner, 1, 0)
    third = jnp.where(inner, 2, 1)
    return top, jnp.where(inner, left_col - 64, left_col + 64), (first, second, third)


def take_window(off_ref, s, ext, win):
    top, shift, tiles = shifts(off_ref, s)
    keep = lax.broadcasted_iota(jnp.int32, (256, 128), 1) < 128 - shift
    for p in range(2):
        a, b, c = [pltpu.roll(ext[p, t, pl.ds(top, 256), :], 128 - shift, 1) for t in tiles]
        win[s, p, :, 0:128] = jnp.where(keep, a, b)
        win[s, p, :, 128:256] = jnp.where(keep, b, c)


def add_window(off_ref, count_ref, s, pair, slide, acc):
    top, shift, (first, second, third) = shifts(off_ref, s)
    lane = lax.broadcasted_iota(jnp.int32, (256, 128), 1)
    before = lane < shift
    active = lane * 0 + s < count_ref[0, 0]
    for p in range(2):
        a, b = [
            pltpu.roll(jnp.where(active, pair[p][:, t * 128 : t * 128 + 128], 0.0), shift, 1) for t in range(2)
        ]
        slide[p, 0, 128:384] = jnp.where(before, 0.0, a)
        slide[p, 1, 128:384] = jnp.where(before, a, b)
        slide[p, 2, 128:384] = jnp.where(before, b, 0.0)
    inner = first == 0
    source = (jnp.where(inner, 0, 1), jnp.where(inner, 1, 2), jnp.where(inner, 2, 0))
    for p in range(2):
        for t in range(3):
            acc[p, t] += slide[p, source[t], pl.ds(128 - top, 384), :]


def each_slot(fn):
    for s in range(MAXPOS):
        fn(s)


def program_kernel(
    count_ref, off_hbm, obj_hbm, probe_hbm, inten_hbm, tab_hbm, obj_out, probe_out,
    tab, inten, ext1, ext2, acc1, acc2, gp, slides, win1, win2, moved, back, mids, probe,
    rows, cols, corners, edge_sems, pair, made, parts, cross, whole, sum_sems, local_sems, off_ref, obj0, probe0,
):
    p = Place()
    ready = greet(p)
    edges = (rows, cols, corners, edge_sems)
    loads = []
    for k, ext in enumerate((ext1, ext2)):
        for t in range(2):
            src = obj_hbm.at[2 * k : 2 * k + 2, :, t * 128 : t * 128 + 128]
            loads.append(pltpu.make_async_copy(src, ext.at[:, t, 64:320], local_sems.at[2 * k + t]))
    loads.append(pltpu.make_async_copy(probe_hbm, probe, local_sems.at[4]))
    loads.append(pltpu.make_async_copy(tab_hbm, tab, local_sems.at[5]))
    loads.append(pltpu.make_async_copy(inten_hbm, inten, local_sems.at[6]))
    loads.append(pltpu.make_async_copy(off_hbm, off_ref, local_sems.at[7]))
    loads.append(pltpu.make_async_copy(obj_hbm, obj0, local_sems.at[8]))
    loads.append(pltpu.make_async_copy(probe_hbm, probe0, local_sems.at[9]))
    for load in loads:
        load.start()
    core1 = lambda t, r0, r1: ext1[:, t, 64 + r0 : 64 + r1]
    core2 = lambda t, r0, r1: ext2[:, t, 64 + r0 : 64 + r1]
    loads[0].wait()
    loads[1].wait()
    send_halo(exchange(p, edges, 0), core1, ready)
    loads[2].wait()
    loads[3].wait()
    send_halo(exchange(p, edges, 1), core2)
    slides[...] = jnp.zeros_like(slides)
    for load in loads[4:]:
        load.wait()

    def reorder(s, carry):
        inten[s] = into_paired_order(tab, inten[s])
        return carry

    lax.fori_loop(0, MAXPOS, reorder, 0)
    unpack_halo(exchange(p, edges, 0), ext1)

    def iteration(it, carry):
        acc1[...] = jnp.zeros_like(acc1)
        acc2[...] = jnp.zeros_like(acc2)
        gp[...] = jnp.zeros_like(gp)

        def forward(s):
            take_window(off_ref, s, ext1, win1)
            pr, pi, wr, wi = probe[0], probe[1], win1[s, 0], win1[s, 1]
            moved[s, 0], moved[s, 1] = propagate(tab, pr * wr - pi * wi, pr * wi + pi * wr, mids.at[s])

        def detector(s):
            take_window(off_ref, s, ext2, win2)
            er = moved[s, 0] * win2[s, 0] - moved[s, 1] * win2[s, 1]
            ei = moved[s, 0] * win2[s, 1] + moved[s, 1] * win2[s, 0]
            fr, fi = combine(*hartley(tab, 3, er, ei, mids.at[s]))
            misfit = fr * fr + fi * fi - inten[s]
            wr, wi = combine(misfit * fr, -(misfit * fi))
            cr, ci = hartley(tab, 4, wr, wi, mids.at[s])
            back[s, 0] = win2[s, 0] * cr - win2[s, 1] * ci
            back[s, 1] = win2[s, 0] * ci + win2[s, 1] * cr
            g2 = (moved[s, 0] * cr - moved[s, 1] * ci, -(moved[s, 0] * ci + moved[s, 1] * cr))
            add_window(off_ref, count_ref, s, g2, slides.at[s % 2], acc2)

        def adjoint(s):
            wr, wi = propagate(tab, back[s, 0], back[s, 1], mids.at[s])
            back[s, 0], back[s, 1] = wr, wi
            active = lax.broadcasted_iota(jnp.int32, (256, 128), 1) * 0 + s < count_ref[0, 0]
            sums = (win1[s, 0] * wr - win1[s, 1] * wi, -(win1[s, 0] * wi + win1[s, 1] * wr))
            for h in range(2):
                for t in range(2):
                    part = jnp.where(active, sums[h][:, t * 128 : t * 128 + 128], 0.0)
                    gp[h, 2 * t : 2 * t + 2] += part.reshape(2, 4, 32, 128)

        def first_slice(s):
            wr, wi = back[s, 0], back[s, 1]
            g1 = (probe[0] * wr - probe[1] * wi, -(probe[0] * wi + probe[1] * wr))
            add_window(off_ref, count_ref, s, g1, slides.at[s % 2], acc1)

        each_slot(forward)
        unpack_halo(exchange(p, edges, 4 * it + 1), ext2)
        each_slot(detector)
        fold2, fold1 = exchange(p, edges, 4 * it + 2), exchange(p, edges, 4 * it + 3)
        send_fold(fold2, acc2)
        each_slot(adjoint)

        bufs = [ref.at[it] for ref in (pair, made, parts, cross, whole)]
        s = Summer(p, gp, bufs, (sum_sems.at[it, 0], sum_sems.at[it, 1]))
        s.begin()
        each_slot(first_slice)
        s.over_plane()
        send_fold(fold1, acc1)
        rate = step_size(probe)
        descend_own(acc2, ext2, rate)
        descend_own(acc1, ext1, rate)
        descend(fold2, ext2, rate)
        s.over_x()
        s.spread()
        descend(fold1, ext1, rate)

        @pl.when(it == 0)
        def _():
            send_halo(exchange(p, edges, 4), core1)
            send_halo(exchange(p, edges, 5), core2)

        s.gather_pair()

        @pl.when(it == 0)
        def _():
            unpack_halo(exchange(p, edges, 4), ext1)

        s.finish()
        for h in range(2):
            for t in range(2):
                lanes = slice(t * 128, t * 128 + 128)
                change = (probe_rate / (NTY * NTX)) * s.whole[h, 2 * t : 2 * t + 2].reshape(256, 128)
                probe[h, :, lanes] -= change
        return carry

    lax.fori_loop(0, ITERS, iteration, 0)
    for t in range(2):
        lanes = slice(t * 128, t * 128 + 128)
        obj_out[0:2, :, lanes] = obj0[0:2, :, lanes] - ext1[:, t, 64:320]
        obj_out[2:4, :, lanes] = obj0[2:4, :, lanes] - ext2[:, t, 64:320]
    probe_out[...] = probe0[...] - probe[...]
    for it in range(SUMS):
        bufs = [ref.at[it] for ref in (pair, made, parts, cross, whole)]
        Summer(p, gp, bufs, (sum_sems.at[it, 0], sum_sems.at[it, 1])).sent()
    for i in range(EXCHANGES):
        wait_sent(exchange(p, edges, i))


def step_size(probe):
    power = probe[0] * probe[0] + probe[1] * probe[1]
    peak = jnp.max(power, axis=(0, 1), keepdims=True) + 1e-06
    return object_rate / peak


def run(count, off, obj, probe, inten, tab):
    smem = pl.BlockSpec(memory_space=pltpu.SMEM)
    anywhere = pl.BlockSpec(memory_space=pltpu.HBM)
    vm = pltpu.VMEM
    slots = vm((MAXPOS, 2, 256, 256), f32)
    return pl.pallas_call(
        program_kernel,
        out_shape=(jax.ShapeDtypeStruct((4, 256, 256), f32), jax.ShapeDtypeStruct((2, 256, 256), f32)),
        in_specs=[smem] + [anywhere] * 5,
        out_specs=(V, V),
        scratch_shapes=[
            vm((6, 2, 256, 256), bf),
            vm((MAXPOS, 256, 256), f32),
            vm((2, 3, 384, 128), f32),
            vm((2, 3, 384, 128), f32),
            vm((2, 3, 384, 128), f32),
            vm((2, 3, 384, 128), f32),
            vm((2, 4, 4, 32, 128), f32),
            vm((2, 2, 3, 512, 128), f32),
            slots,
            slots,
            slots,
            slots,
            slots,
            vm((2, 256, 256), f32),
            vm((EXCHANGES, 2, 2, 2, 2, 64, 128), f32),
            vm((EXCHANGES, 2, 2, 2, 128, 128), f32),
            vm((EXCHANGES, 2, 4, 2, 32, 128), f32),
            pltpu.SemaphoreType.DMA((EXCHANGES, 2, 8)),
            vm((SUMS, 4, 4, 32, 128), f32),
            vm((SUMS, 4, 4, 32, 128), f32),
            vm((SUMS, 4, 4, 32, 128), f32),
            vm((SUMS, 4, 32, 128), f32),
            vm((SUMS, 2, 4, 4, 32, 128), f32),
            pltpu.SemaphoreType.DMA((SUMS, 2, 48)),
            pltpu.SemaphoreType.DMA((10,)),
            pltpu.SMEM((2, MAXPOS), jnp.int32),
            vm((4, 256, 256), f32),
            vm((2, 256, 256), f32),
        ],
        compiler_params=pltpu.CompilerParams(collective_id=0, has_side_effects=True, vmem_limit_bytes=60 << 20),
        name="iterations",
    )(count, off, obj, probe, inten, tab)


def body(object_slices, probe, position_count, offsets, intensities):
    obj_change, probe_change = run(
        position_count,
        offsets[0, 0].T,
        object_slices.reshape(4, 256, 256),
        probe,
        intensities[0, 0],
        jnp.asarray(tables()),
    )
    return object_slices - obj_change.reshape(2, 2, 256, 256), probe - probe_change


def solution(mesh):
    placed = (
        P(None, None, "ty", "tx"),
        P(),
        P("ty", "tx"),
        P("ty", "tx", None, None),
        P("ty", "tx", None, None, None),
    )
    return jax.shard_map(
        body,
        mesh=mesh,
        in_specs=placed,
        out_specs=(P(None, None, "ty", "tx"), P()),
        check_vma=False,
    )
```

time: 126 us -> 109 us (0.87)
  Pallas kernels: 119 us -> 104 us
  local copies, waits for them, and re-layouts: 2.94 us -> 0.01 us
  other arithmetic: 1.97 us -> 3.28 us
    pallas_call x1, Pallas kernels: 119 us -> 104 us  [run(): pl.pallas_call(program_kernel, out_shape=(jax.ShapeDtypeStruct((4, 256, 2...]
    unnamed x6, local copies, waits for them, and re-layouts: 2.94 us -> 0.01 us
    sub x1, other arithmetic: 1.11 us -> 2.42 us  [body(): object_slices - obj_change.reshape(2, 2, 256, 256)]
where the time goes in v4:
time: 109 us
  Pallas kernels  104 us (95%)
  other arithmetic  3.28 us (3%)
  between operations  1.32 us (1%)
    pallas_call x1, Pallas kernels, run(): pl.pallas_call(program_kernel, out_shape=(jax.ShapeDtypeStruct((4, 256, 2...  104 us
    sub x1, other arithmetic, body(): object_slices - obj_change.reshape(2, 2, 256, 256)  2.42 us

profile of v4, /device:TPU:1, one launch (start us, length us, event | category | flops | bytes accessed | tf_op | source)
XLA Modules:
  0.0 108.7 jit_solution(6028857938065770471)
XLA Ops:
  1.3 0.0 copy-start
  1.3 104.1 %iterations.1 = (f32[4,256,256]{2,1,0:T(8,128)}, f32[2,256,256]{2,1,0:T(8,128)}) custom-call(s32[1,1]{1,0:T(1,128)S(6)} %copy.8.count_ref, s32[2,5]{1,0:T(2,128)} %bitcast.9, f32[4,256,256]{2,1,0:T(8,128)} %bitcast.6, f32[2,256,256]{2,1,0:T(8,128)} %probe_hbm.1, f32[5,256,256]{2,1,0:T(8,128)} %bitcast.7, bf16[6,2,256,256]{3,2,1,0:T(8,128)(2,1)} %constant.2.clone.tab_hbm), custom_call_target="tpu_custom_call" | custom-call | tf_op jit(solution)/shard_map/iterations/pallas_call | solution.py:565
  105.4 0.0 copy-done
  105.4 0.0 copy-start.1
  105.4 0.0 copy-start.2
  105.4 2.4 %sub.6 = f32[2,2,256,256]{3,2,1,0:T(8,128)} subtract(f32[2,2,256,256]{3,2,1,0:T(8,128)S(1)} %copy-done, f32[2,2,256,256]{3,2,1,0:T(8,128)} %bitcast.8) | non-fusion elementwise | flops 262144 | bytes 3145728 | tf_op jit(solution)/shard_map/sub | solution.py:614
  107.8 0.0 copy-done.1
  107.8 0.0 copy-done.2
  107.8 0.9 sub.7
Async XLA Ops:
  1.3 104.1 %copy-start = (f32[2,2,256,256]{3,2,1,0:T(8,128)S(1)}, f32[2,2,256,256]{3,2,1,0:T(8,128)}, u32[]{:S(2)}) copy-start(f32[2,2,256,256]{3,2,1,0:T(8,128)} %param.6) | copy-start | bytes 3145732
  105.4 2.4 %copy-start.1 = (f32[2,256,256]{2,1,0:T(8,128)S(1)}, f32[2,256,256]{2,1,0:T(8,128)}, u32[]{:S(2)}) copy-start(f32[2,256,256]{2,1,0:T(8,128)} %probe_hbm.1) | copy-start | bytes 1572868
  105.4 2.4 %copy-start.2 = (f32[2,256,256]{2,1,0:T(8,128)S(1)}, f32[2,256,256]{2,1,0:T(8,128)}, u32[]{:S(2)}) copy-start(f32[2,256,256]{2,1,0:T(8,128)} %get-tuple-element.5) | copy-start | bytes 1572868

commit v5 on v4

--- a/solution.py
+++ b/solution.py
@@ -320,6 +320,11 @@
         self.cross[self.p.x] = total
         for k in (2, 1, 3):
             self.x_copy(k).start()
+        for k in range(4):
+            self.pair_copy(k).wait_send()
+            for j in range(4):
+                if k or j:
+                    self.plane_copy(k, j).wait_send()
 
     def spread(self):
         for k in (1, 3, 2):
@@ -332,26 +337,25 @@
                     self.back_copy(k, j).start()
 
     def gather_pair(self):
+        for k in (1, 2, 3):
+            self.x_copy(k).wait_send()
         for k in (0, 1, 3, 2):
             for j in range(4):
                 if k or j:
                     self.back_copy(k, j).wait_recv()
             self.forward_copy(k).start()
+        for k in range(4):
+            for j in range(4):
+                if k or j:
+                    self.back_copy(k, j).wait_send()
 
     def finish(self):
         for k in range(4):
             self.forward_copy(k).wait_recv()
-            self.pair_copy(k).wait_send()
 
     def sent(self):
         for k in range(4):
             self.forward_copy(k).wait_send()
-            for j in range(4):
-                if k or j:
-                    self.plane_copy(k, j).wait_send()
-                    self.back_copy(k, j).wait_send()
-        for k in (1, 2, 3):
-            self.x_copy(k).wait_send()
 
 
 def greet(p):
@@ -423,7 +427,7 @@
 def program_kernel(
     count_ref, off_hbm, obj_hbm, probe_hbm, inten_hbm, tab_hbm, obj_out, probe_out,
     tab, inten, ext1, ext2, acc1, acc2, gp, slides, win1, win2, moved, back, mids, probe,
-    rows, cols, corners, edge_sems, pair, made, parts, cross, whole, sum_sems, local_sems, off_ref, obj0, probe0,
+    rows, cols, corners, edge_sems, pair, made, parts, cross, whole, sum_sems, local_sems, off_ref,
 ):
     p = Place()
     ready = greet(p)
@@ -437,8 +441,6 @@
     loads.append(pltpu.make_async_copy(tab_hbm, tab, local_sems.at[5]))
     loads.append(pltpu.make_async_copy(inten_hbm, inten, local_sems.at[6]))
     loads.append(pltpu.make_async_copy(off_hbm, off_ref, local_sems.at[7]))
-    loads.append(pltpu.make_async_copy(obj_hbm, obj0, local_sems.at[8]))
-    loads.append(pltpu.make_async_copy(probe_hbm, probe0, local_sems.at[9]))
     for load in loads:
         load.start()
     core1 = lambda t, r0, r1: ext1[:, t, 64 + r0 : 64 + r1]
@@ -449,7 +451,8 @@
     loads[2].wait()
     loads[3].wait()
     send_halo(exchange(p, edges, 1), core2)
-    slides[...] = jnp.zeros_like(slides)
+    for ref in (slides, acc1, acc2, gp):
+        ref[...] = jnp.zeros_like(ref)
     for load in loads[4:]:
         load.wait()
 
@@ -460,10 +463,13 @@
     lax.fori_loop(0, MAXPOS, reorder, 0)
     unpack_halo(exchange(p, edges, 0), ext1)
 
+    stores = []
+    for k, ext in enumerate((ext1, ext2)):
+        for t in range(2):
+            dst = obj_out.at[2 * k : 2 * k + 2, :, t * 128 : t * 128 + 128]
+            stores.append(pltpu.make_async_copy(ext.at[:, t, 64:320], dst, local_sems.at[8 + 2 * k + t]))
+
     def iteration(it, carry):
-        acc1[...] = jnp.zeros_like(acc1)
-        acc2[...] = jnp.zeros_like(acc2)
-        gp[...] = jnp.zeros_like(gp)
 
         def forward(s):
             take_window(off_ref, s, ext1, win1)
@@ -514,7 +520,17 @@
         rate = step_size(probe)
         descend_own(acc2, ext2, rate)
         descend_own(acc1, ext1, rate)
+        acc1[...] = jnp.zeros_like(acc1)
+        acc2[...] = jnp.zeros_like(acc2)
+        for i in range(3):
+            wait_sent(exchange(p, edges, 4 * it + i))
         descend(fold2, ext2, rate)
+
+        @pl.when(it == ITERS - 1)
+        def _():
+            stores[2].start()
+            stores[3].start()
+
         s.over_x()
         s.spread()
         descend(fold1, ext1, rate)
@@ -524,31 +540,32 @@
             send_halo(exchange(p, edges, 4), core1)
             send_halo(exchange(p, edges, 5), core2)
 
+        @pl.when(it == ITERS - 1)
+        def _():
+            stores[0].start()
+            stores[1].start()
+
+        wait_sent(fold1)
         s.gather_pair()
 
         @pl.when(it == 0)
         def _():
             unpack_halo(exchange(p, edges, 4), ext1)
 
+        gp[...] = jnp.zeros_like(gp)
         s.finish()
         for h in range(2):
             for t in range(2):
                 lanes = slice(t * 128, t * 128 + 128)
                 change = (probe_rate / (NTY * NTX)) * s.whole[h, 2 * t : 2 * t + 2].reshape(256, 128)
                 probe[h, :, lanes] -= change
+        s.sent()
         return carry
 
     lax.fori_loop(0, ITERS, iteration, 0)
-    for t in range(2):
-        lanes = slice(t * 128, t * 128 + 128)
-        obj_out[0:2, :, lanes] = obj0[0:2, :, lanes] - ext1[:, t, 64:320]
-        obj_out[2:4, :, lanes] = obj0[2:4, :, lanes] - ext2[:, t, 64:320]
-    probe_out[...] = probe0[...] - probe[...]
-    for it in range(SUMS):
-        bufs = [ref.at[it] for ref in (pair, made, parts, cross, whole)]
-        Summer(p, gp, bufs, (sum_sems.at[it, 0], sum_sems.at[it, 1])).sent()
-    for i in range(EXCHANGES):
-        wait_sent(exchange(p, edges, i))
+    probe_out[...] = probe[...]
+    for store in stores:
+        store.wait()
 
 
 def step_size(probe):
@@ -566,7 +583,7 @@
         program_kernel,
         out_shape=(jax.ShapeDtypeStruct((4, 256, 256), f32), jax.ShapeDtypeStruct((2, 256, 256), f32)),
         in_specs=[smem] + [anywhere] * 5,
-        out_specs=(V, V),
+        out_specs=(anywhere, V),
         scratch_shapes=[
             vm((6, 2, 256, 256), bf),
             vm((MAXPOS, 256, 256), f32),
@@ -592,10 +609,8 @@
             vm((SUMS, 4, 32, 128), f32),
             vm((SUMS, 2, 4, 4, 32, 128), f32),
             pltpu.SemaphoreType.DMA((SUMS, 2, 48)),
-            pltpu.SemaphoreType.DMA((10,)),
+            pltpu.SemaphoreType.DMA((12,)),
             pltpu.SMEM((2, MAXPOS), jnp.int32),
-            vm((4, 256, 256), f32),
-            vm((2, 256, 256), f32),
         ],
         compiler_params=pltpu.CompilerParams(collective_id=0, has_side_effects=True, vmem_limit_bytes=60 << 20),
         name="iterations",
@@ -603,7 +618,7 @@
 
 
 def body(object_slices, probe, position_count, offsets, intensities):
-    obj_change, probe_change = run(
+    obj, probe = run(
         position_count,
         offsets[0, 0].T,
         object_slices.reshape(4, 256, 256),
@@ -611,7 +626,7 @@
         intensities[0, 0],
         jnp.asarray(tables()),
     )
-    return object_slices - obj_change.reshape(2, 2, 256, 256), probe - probe_change
+    return obj.reshape(2, 2, 256, 256), probe
 
 
 def solution(mesh):

time: 109 us -> 108 us (level)
  other arithmetic: 3.28 us -> 0 us
  local copies, waits for them, and re-layouts: 0.01 us -> 3.14 us
    sub x2 -> x0, other arithmetic: 3.28 us -> none  [the longest x1 2.42 us: body(): object_slices - obj_change.reshape(2, 2, 256, 256)]
    unnamed x6 -> x4, local copies, waits for them, and re-layouts: 0.01 us -> 3.14 us
where the time goes in v5:
time: 108 us
  Pallas kernels  104 us (96%)
  local copies, waits for them, and re-layouts  3.14 us (3%)
  between operations  1.29 us (1%)
    pallas_call x1, Pallas kernels, run(): pl.pallas_call(program_kernel, out_shape=(jax.ShapeDtypeStruct((4, 256, 2...  104 us
    unnamed x4, local copies, waits for them, and re-layouts  3.14 us

profile of v5, /device:TPU:1, one launch (start us, length us, event | category | flops | bytes accessed | tf_op | source)
XLA Modules:
  0.0 108.1 jit_solution(5333596077651990438)
XLA Ops:
  1.3 103.6 %iterations.1 = (f32[4,256,256]{2,1,0:T(8,128)}, f32[2,256,256]{2,1,0:T(8,128)}) custom-call(s32[1,1]{1,0:T(1,128)S(6)} %copy.10.count_ref, s32[2,5]{1,0:T(2,128)} %bitcast.9, f32[4,256,256]{2,1,0:T(8,128)} %bitcast.8, f32[2,256,256]{2,1,0:T(8,128)} %probe_hbm.1, f32[5,256,256]{2,1,0:T(8,128)} %bitcast.6, bf16[6,2,256,256]{3,2,1,0:T(8,128)(2,1)} %constant.2.clone.tab_hbm), custom_call_target="tpu_custom_call" | custom-call | tf_op jit(solution)/shard_map/iterations/pallas_call | solution.py:582
  104.9 0.0 copy-start
  104.9 2.3 %copy.11 = f32[2,2,256,256]{3,2,1,0:T(8,128)} copy(f32[2,2,256,256]{3,2,1,0:T(8,128)} %bitcast.7) | data formatting | bytes 2097152
  107.3 0.0 copy-done
  107.3 0.8 copy.12
Async XLA Ops:
  104.9 2.4 %copy-start = (f32[2,256,256]{2,1,0:T(8,128)S(1)}, f32[2,256,256]{2,1,0:T(8,128)}, u32[]{:S(2)}) copy-start(f32[2,256,256]{2,1,0:T(8,128)} %get-tuple-element.9) | copy-start | bytes 1572868

commit v6 on v5

--- a/solution.py
+++ b/solution.py
@@ -583,7 +583,7 @@
         program_kernel,
         out_shape=(jax.ShapeDtypeStruct((4, 256, 256), f32), jax.ShapeDtypeStruct((2, 256, 256), f32)),
         in_specs=[smem] + [anywhere] * 5,
-        out_specs=(anywhere, V),
+        out_specs=(pl.BlockSpec(memory_space=pl.ANY), V),
         scratch_shapes=[
             vm((6, 2, 256, 256), bf),
             vm((MAXPOS, 256, 256), f32),
@@ -612,9 +612,9 @@
             pltpu.SemaphoreType.DMA((12,)),
             pltpu.SMEM((2, MAXPOS), jnp.int32),
         ],
-        compiler_params=pltpu.CompilerParams(collective_id=0, has_side_effects=True, vmem_limit_bytes=60 << 20),
+        compiler_params=pltpu.CompilerParams(collective_id=0, has_side_effects=True, vmem_limit_bytes=50 << 20),
         name="iterations",
-    )(count, off, obj, probe, inten, tab)
+    )(count, *[pltpu.with_memory_space_constraint(x, pltpu.HBM) for x in (off, obj, probe, inten, tab)])
 
 
 def body(object_slices, probe, position_count, offsets, intensities):

time: 108 us -> 106 us (0.981)
  local copies, waits for them, and re-layouts: 3.14 us -> 1.77 us
    unnamed x4 -> x2, local copies, waits for them, and re-layouts: 3.14 us -> 1.77 us
where the time goes in v6:
time: 106 us
  Pallas kernels  103 us (97%)
  local copies, waits for them, and re-layouts  1.77 us (2%)
  between operations  1.28 us (1%)
    pallas_call x1, Pallas kernels, run(): pl.pallas_call(program_kernel, out_shape=(jax.ShapeDtypeStruct((4, 256, 2...  103 us

profile of v6, /device:TPU:1, one launch (start us, length us, event | category | flops | bytes accessed | tf_op | source)
XLA Modules:
  0.0 105.9 jit_solution(5835738240729851886)
XLA Ops:
  1.3 102.9 %iterations.1 = (f32[4,256,256]{2,1,0:T(8,128)S(1)}, f32[2,256,256]{2,1,0:T(8,128)S(1)}) custom-call(s32[1,1]{1,0:T(1,128)S(6)} %copy.10.count_ref, s32[2,5]{1,0:T(2,128)} %bitcast.9, f32[4,256,256]{2,1,0:T(8,128)} %bitcast.8, f32[2,256,256]{2,1,0:T(8,128)} %probe_hbm.1, f32[5,256,256]{2,1,0:T(8,128)} %bitcast.7, bf16[6,2,256,256]{3,2,1,0:T(8,128)(2,1)} %constant.2.clone.tab_hbm), custom_call_target="tpu_custom_call" | custom-call | tf_op jit(solution)/shard_map/iterations/pallas_call | solution.py:582
  104.1 1.0 copy.11
  105.1 0.8 copy.12

commit v7 on v6

--- a/solution.py
+++ b/solution.py
@@ -110,7 +110,7 @@
 
 NTY, NTX = 8, 16
 MESH = pl.DeviceIdType.MESH
-DIRS = [(dy, dx) for dy in (-1, 0, 1) for dx in (-1, 0, 1) if (dy, dx) != (0, 0)]
+DIRS = [(1, 0), (-1, 0), (0, 1), (0, -1)]
 V = pl.BlockSpec(memory_space=pltpu.VMEM)
 
 
@@ -171,96 +171,87 @@
 
 
 class Edges:
-    def __init__(self, place, rows, cols, corners, sems):
-        self.place, self.rows, self.cols, self.corners = place, rows, cols, corners
+    def __init__(self, place, bufs, sems):
+        self.place, self.bufs = place, bufs
         self.send, self.recv = sems
 
-    def slot(self, bufs, dy, dx):
-        if dx == 0:
-            return bufs[0].at[(dy + 1) // 2]
-        if dy == 0:
-            return bufs[1].at[(dx + 1) // 2]
-        return bufs[2].at[(dy + 1) + (dx + 1) // 2]
-
-    def out(self, dy, dx):
-        return self.slot((self.rows[0], self.cols[0], self.corners[0]), dy, dx)
-
-    def inc(self, dy, dx):
-        return self.slot((self.rows[1], self.cols[1], self.corners[1]), dy, dx)
-
-    def copy(self, dy, dx):
-        i = DIRS.index((dy, dx))
-        return remote(self.out(dy, dx), self.inc(dy, dx), self.send.at[i], self.recv.at[i], self.place.neighbour(dy, dx))
-
-
-ORDER = [(1, 1), (1, -1), (-1, 1), (-1, -1), (0, 1), (0, -1), (1, 0), (-1, 0)]
-
-
-def send_halo(e, core, ready=None):
-    for dy, dx in ORDER:
-        r0, r1 = {-1: (0, 64), 0: (0, 256), 1: (192, 256)}[dy]
-        if dx == 0:
-            for t in range(2):
-                e.out(dy, dx)[:, t] = core(t, r0, r1)
-        else:
-            e.out(dy, dx)[...] = pack(core((dx + 1) // 2, r0, r1), dx)
-        if ready is None:
-            e.copy(dy, dx).start()
-    if ready is not None:
-        ready()
-        for dy, dx in ORDER:
-            e.copy(dy, dx).start()
-
-
-def unpack_halo(e, ext):
-    for dy in (-1, 1):
-        e.copy(dy, 0).wait_recv()
-        r0 = 320 if dy < 0 else 0
-        for t in range(2):
-            ext[:, t, r0 : r0 + 64] = e.inc(dy, 0)[:, t]
-    for dy in (0, -1, 1):
-        e.copy(dy, -1).wait_recv()
-        e.copy(dy, 1).wait_recv()
-        r0, r1 = {-1: (320, 384), 0: (64, 320), 1: (0, 64)}[dy]
-        left, right = unpack(e.inc(dy, -1)[...], -1), unpack(e.inc(dy, 1)[...], 1)
-        ext[:, 2, r0:r1] = jnp.where(half_lanes(left.shape), left, right)
+    def slot(self, kind, way, d):
+        return self.bufs[kind].at[way, (d + 1) // 2]
+
+    def copy(self, kind, d):
+        i = 2 * kind + (d + 1) // 2
+        device = self.place.neighbour(0, d) if kind == COLS else self.place.neighbour(d, 0)
+        src, dst = self.slot(kind, 0, d), self.slot(kind, 1, d)
+        return remote(src, dst, self.send.at[i], self.recv.at[i], device)
+
+    def post(self, kind, d, values):
+        self.slot(kind, 0, d)[...] = values
+        self.copy(kind, d).start()
+
+    def get(self, kind, d):
+        self.copy(kind, d).wait_recv()
+        return self.slot(kind, 1, d)[...]
+
+
+ROWS, COLS, STRIPS = 0, 1, 2
+
+
+def send_halo(e, ext):
+    for d in (1, -1):
+        e.post(COLS, d, pack(ext[:, (d + 1) // 2, 64:320], d))
+    for d in (1, -1):
+        r0 = 256 if d > 0 else 64
+        e.post(ROWS, d, ext[:, 0:2, r0 : r0 + 64])
+
+
+def halo_strips(e, ext):
+    left, right = unpack(e.get(COLS, -1), -1), unpack(e.get(COLS, 1), 1)
+    ext[:, 2, 64:320] = jnp.where(half_lanes(left.shape), left, right)
+    for d in (1, -1):
+        r0 = 256 if d > 0 else 64
+        e.post(STRIPS, d, ext[:, 2, r0 : r0 + 64])
+
+
+def finish_halo(e, ext):
+    for d in (1, -1):
+        r0 = 320 if d < 0 else 0
+        ext[:, 0:2, r0 : r0 + 64] = e.get(ROWS, d)
+    for d in (1, -1):
+        r0 = 320 if d < 0 else 0
+        ext[:, 2, r0 : r0 + 64] = e.get(STRIPS, d)
 
 
 def send_fold(e, g):
-    for dy, dx in ORDER:
-        r0, r1 = {-1: (0, 64), 0: (64, 320), 1: (320, 384)}[dy]
-        if dx == 0:
-            for t in range(2):
-                e.out(dy, dx)[:, t] = g[:, t, r0:r1]
-        else:
-            e.out(dy, dx)[...] = pack(g[:, 2, r0:r1], -dx)
-        e.copy(dy, dx).start()
-
-
-def step_down(ext, t, r0, r1, change):
-    ext[:, t, 64 + r0 : 64 + r1] -= change
+    for kind, t in ((STRIPS, 2), (ROWS, slice(0, 2))):
+        for d in (1, -1):
+            r0 = 320 if d > 0 else 0
+            e.post(kind, d, g[:, t, r0 : r0 + 64])
+
+
+def fold_columns(e, g):
+    for d in (1, -1):
+        r0 = 64 if d > 0 else 256
+        g[:, 2, r0 : r0 + 64] += e.get(STRIPS, d)
+    for d in (1, -1):
+        e.post(COLS, d, pack(g[:, 2, 64:320], -d))
 
 
 def descend_own(g, ext, rate):
-    for t in range(2):
-        step_down(ext, t, 0, 256, rate * g[:, t, 64:320])
+    ext[:, 0:2, 64:320] -= rate * g[:, 0:2, 64:320]
 
 
 def descend(e, ext, rate):
-    for dy, dx in ORDER[4:] + ORDER[:4]:
-        e.copy(dy, dx).wait_recv()
-        r0, r1 = {-1: (192, 256), 0: (0, 256), 1: (0, 64)}[dy]
-        if dx == 0:
-            for t in range(2):
-                step_down(ext, t, r0, r1, rate * e.inc(dy, dx)[:, t])
-        else:
-            values = keep_side(unpack(e.inc(dy, dx)[...], -dx), -dx)
-            step_down(ext, (1 - dx) // 2, r0, r1, rate * values)
+    for d in (1, -1):
+        r0 = 64 if d > 0 else 256
+        ext[:, 0:2, r0 : r0 + 64] -= rate * e.get(ROWS, d)
+    for d in (1, -1):
+        ext[:, (1 - d) // 2, 64:320] -= rate * keep_side(unpack(e.get(COLS, d), -d), -d)
 
 
 def wait_sent(e):
-    for dy, dx in ORDER:
-        e.copy(dy, dx).wait_send()
+    for kind in (ROWS, COLS, STRIPS):
+        for d in (1, -1):
+            e.copy(kind, d).wait_send()
 
 
 class Summer:
@@ -377,9 +368,8 @@
 
 
 def exchange(p, refs, i):
-    rows, cols, corners, sems = [ref.at[i] for ref in refs]
-    pair = lambda ref: (ref.at[0], ref.at[1])
-    return Edges(p, pair(rows), pair(cols), pair(corners), pair(sems))
+    rows, cols, strips, sems = [ref.at[i] for ref in refs]
+    return Edges(p, (rows, cols, strips), (sems.at[0], sems.at[1]))
 
 
 def shifts(off_ref, s):
@@ -427,11 +417,11 @@
 def program_kernel(
     count_ref, off_hbm, obj_hbm, probe_hbm, inten_hbm, tab_hbm, obj_out, probe_out,
     tab, inten, ext1, ext2, acc1, acc2, gp, slides, win1, win2, moved, back, mids, probe,
-    rows, cols, corners, edge_sems, pair, made, parts, cross, whole, sum_sems, local_sems, off_ref,
+    rows, cols, strips, edge_sems, pair, made, parts, cross, whole, sum_sems, local_sems, off_ref,
 ):
     p = Place()
     ready = greet(p)
-    edges = (rows, cols, corners, edge_sems)
+    edges = (rows, cols, strips, edge_sems)
     loads = []
     for k, ext in enumerate((ext1, ext2)):
         for t in range(2):
@@ -443,25 +433,28 @@
     loads.append(pltpu.make_async_copy(off_hbm, off_ref, local_sems.at[7]))
     for load in loads:
         load.start()
-    core1 = lambda t, r0, r1: ext1[:, t, 64 + r0 : 64 + r1]
-    core2 = lambda t, r0, r1: ext2[:, t, 64 + r0 : 64 + r1]
     loads[0].wait()
     loads[1].wait()
-    send_halo(exchange(p, edges, 0), core1, ready)
+    ready()
+    send_halo(exchange(p, edges, 0), ext1)
     loads[2].wait()
     loads[3].wait()
-    send_halo(exchange(p, edges, 1), core2)
+    send_halo(exchange(p, edges, 1), ext2)
     for ref in (slides, acc1, acc2, gp):
         ref[...] = jnp.zeros_like(ref)
     for load in loads[4:]:
         load.wait()
 
+    halo_strips(exchange(p, edges, 0), ext1)
+    for s in range(2):
+        inten[s] = into_paired_order(tab, inten[s])
+    finish_halo(exchange(p, edges, 0), ext1)
+
     def reorder(s, carry):
         inten[s] = into_paired_order(tab, inten[s])
         return carry
 
-    lax.fori_loop(0, MAXPOS, reorder, 0)
-    unpack_halo(exchange(p, edges, 0), ext1)
+    lax.fori_loop(2, MAXPOS, reorder, 0)
 
     stores = []
     for k, ext in enumerate((ext1, ext2)):
@@ -504,12 +497,21 @@
             g1 = (probe[0] * wr - probe[1] * wi, -(probe[0] * wi + probe[1] * wr))
             add_window(off_ref, count_ref, s, g1, slides.at[s % 2], acc1)
 
-        each_slot(forward)
-        unpack_halo(exchange(p, edges, 4 * it + 1), ext2)
+        for s in range(3):
+            forward(s)
+        halo2 = exchange(p, edges, 4 * it + 1)
+        halo_strips(halo2, ext2)
+        for s in range(3, MAXPOS):
+            forward(s)
+        finish_halo(halo2, ext2)
         each_slot(detector)
         fold2, fold1 = exchange(p, edges, 4 * it + 2), exchange(p, edges, 4 * it + 3)
         send_fold(fold2, acc2)
-        each_slot(adjoint)
+        for s in range(3):
+            adjoint(s)
+        fold_columns(fold2, acc2)
+        for s in range(3, MAXPOS):
+            adjoint(s)
 
         bufs = [ref.at[it] for ref in (pair, made, parts, cross, whole)]
         s = Summer(p, gp, bufs, (sum_sems.at[it, 0], sum_sems.at[it, 1]))
@@ -520,6 +522,7 @@
         rate = step_size(probe)
         descend_own(acc2, ext2, rate)
         descend_own(acc1, ext1, rate)
+        fold_columns(fold1, acc1)
         acc1[...] = jnp.zeros_like(acc1)
         acc2[...] = jnp.zeros_like(acc2)
         for i in range(3):
@@ -537,8 +540,9 @@
 
         @pl.when(it == 0)
         def _():
-            send_halo(exchange(p, edges, 4), core1)
-            send_halo(exchange(p, edges, 5), core2)
+            send_halo(exchange(p, edges, 4), ext1)
+            send_halo(exchange(p, edges, 5), ext2)
+            halo_strips(exchange(p, edges, 4), ext1)
 
         @pl.when(it == ITERS - 1)
         def _():
@@ -550,7 +554,7 @@
 
         @pl.when(it == 0)
         def _():
-            unpack_halo(exchange(p, edges, 4), ext1)
+            finish_halo(exchange(p, edges, 4), ext1)
 
         gp[...] = jnp.zeros_like(gp)
         s.finish()
@@ -601,8 +605,8 @@
             vm((2, 256, 256), f32),
             vm((EXCHANGES, 2, 2, 2, 2, 64, 128), f32),
             vm((EXCHANGES, 2, 2, 2, 128, 128), f32),
-            vm((EXCHANGES, 2, 4, 2, 32, 128), f32),
-            pltpu.SemaphoreType.DMA((EXCHANGES, 2, 8)),
+            vm((EXCHANGES, 2, 2, 2, 64, 128), f32),
+            pltpu.SemaphoreType.DMA((EXCHANGES, 2, 6)),
             vm((SUMS, 4, 4, 32, 128), f32),
             vm((SUMS, 4, 4, 32, 128), f32),
             vm((SUMS, 4, 4, 32, 128), f32),

time: 106 us -> 126 us (1.19)
  Pallas kernels: 103 us -> 123 us
    pallas_call x1, Pallas kernels: 103 us -> 123 us  [run(): pl.pallas_call(program_kernel, out_shape=(jax.ShapeDtypeStruct((4, 256, 2...]
where the time goes in v7:
time: 126 us
  Pallas kernels  123 us (98%)
  local copies, waits for them, and re-layouts  1.77 us (1%)
  between operations  1.28 us (1%)
    pallas_call x1, Pallas kernels, run(): pl.pallas_call(program_kernel, out_shape=(jax.ShapeDtypeStruct((4, 256, 2...  123 us

profile of v7, /device:TPU:1, one launch (start us, length us, event | category | flops | bytes accessed | tf_op | source)
XLA Modules:
  0.0 125.9 jit_solution(7060282692130482878)
XLA Ops:
  1.3 122.9 %iterations.1 = (f32[4,256,256]{2,1,0:T(8,128)S(1)}, f32[2,256,256]{2,1,0:T(8,128)S(1)}) custom-call(s32[1,1]{1,0:T(1,128)S(6)} %copy.10.count_ref, s32[2,5]{1,0:T(2,128)} %bitcast.9, f32[4,256,256]{2,1,0:T(8,128)} %bitcast.8, f32[2,256,256]{2,1,0:T(8,128)} %probe_hbm.1, f32[5,256,256]{2,1,0:T(8,128)} %bitcast.7, bf16[6,2,256,256]{3,2,1,0:T(8,128)(2,1)} %constant.2.clone.tab_hbm), custom_call_target="tpu_custom_call" | custom-call | tf_op jit(solution)/shard_map/iterations/pallas_call | solution.py:586
  124.2 1.0 copy.11
  125.1 0.8 copy.12

commit v8 on v6

--- a/solution.py
+++ b/solution.py
@@ -516,11 +516,14 @@
         s.begin()
         each_slot(first_slice)
         s.over_plane()
-        send_fold(fold1, acc1)
+
+        @pl.when(it == 0)
+        def _():
+            send_fold(fold1, acc1)
+
         rate = step_size(probe)
         descend_own(acc2, ext2, rate)
         descend_own(acc1, ext1, rate)
-        acc1[...] = jnp.zeros_like(acc1)
         acc2[...] = jnp.zeros_like(acc2)
         for i in range(3):
             wait_sent(exchange(p, edges, 4 * it + i))
@@ -532,6 +535,12 @@
             stores[3].start()
 
         s.over_x()
+
+        @pl.when(it == ITERS - 1)
+        def _():
+            send_fold(fold1, acc1)
+
+        acc1[...] = jnp.zeros_like(acc1)
         s.spread()
         descend(fold1, ext1, rate)
 

time: 106 us -> 107 us (level)
  no operation moved by 1% of the time
where the time goes in v8:
time: 107 us
  Pallas kernels  104 us (97%)
  local copies, waits for them, and re-layouts  1.77 us (2%)
  between operations  1.28 us (1%)
    pallas_call x1, Pallas kernels, run(): pl.pallas_call(program_kernel, out_shape=(jax.ShapeDtypeStruct((4, 256, 2...  104 us

profile of v8, /device:TPU:1, one launch (start us, length us, event | category | flops | bytes accessed | tf_op | source)
XLA Modules:
  0.0 107.0 jit_solution(30675820772153819)
XLA Ops:
  1.3 103.9 %iterations.1 = (f32[4,256,256]{2,1,0:T(8,128)S(1)}, f32[2,256,256]{2,1,0:T(8,128)S(1)}) custom-call(s32[1,1]{1,0:T(1,128)S(6)} %copy.10.count_ref, s32[2,5]{1,0:T(2,128)} %bitcast.9, f32[4,256,256]{2,1,0:T(8,128)} %bitcast.8, f32[2,256,256]{2,1,0:T(8,128)} %probe_hbm.1, f32[5,256,256]{2,1,0:T(8,128)} %bitcast.7, bf16[6,2,256,256]{3,2,1,0:T(8,128)(2,1)} %constant.2.clone.tab_hbm), custom_call_target="tpu_custom_call" | custom-call | tf_op jit(solution)/shard_map/iterations/pallas_call | solution.py:591
  105.2 1.0 copy.11
  106.2 0.8 copy.12
